TPU v7x, 256 devices: a whole 4x4x8 slice. The times are simulated.
256 devices in a mesh: seq: 32 (over x, z_lo, core), head: 8 (over z_hi, y).
Axes of the slice: x: 4, y: 4, z: 8 (z_hi: 2, z_lo: 4; z = z_hi * 4 + z_lo), core: 2. Of those that a mesh axis runs over, the one named last changes fastest.
Arguments:
- queries: bfloat16 [8192, 8192], P('seq', 'head'), may hold values from -4.6 to 4.6
- keys: bfloat16 [8192, 1024], P('seq', 'head'), may hold values from -4.6 to 4.6
- values: bfloat16 [8192, 1024], P('seq', 'head'), may hold values from -4 to 4
- key_keep: int32 [8192], P('seq'), may hold values 0 or 1
- global_positions: int32 [384], replicated, may hold values from 0 to 8191
- gain: bfloat16 [8192], P('head'), may hold values from 0.5 to 1.5
- cotangent: bfloat16 [8192, 8192], P('seq', 'head'), may hold values from -6 to 6
Outputs:
- normed: bfloat16 [8192, 8192], P('seq', 'head')
- query_grad: bfloat16 [8192, 8192], P('seq', 'head')
- key_grad: bfloat16 [8192, 1024], P('seq', 'head')
- value_grad: bfloat16 [8192, 1024], P('seq', 'head')
All inputs are finite; a program needn't handle non-finite values. No bound on the sum of `key_keep` on one device may be relied on, other than what follows from the above.
Results may differ from a plain program's by a relative error of at most 0.018.
Values may be sent and summed in bfloat16 or wider, within the bound.
A program may use at most 64 MiB of HBM per device.

v0:
```python
import jax
import jax.numpy as jnp
from jax import lax
from jax.sharding import Mesh
from jax.sharding import PartitionSpec as P

QH = 64
KVH = 8
HD = 128
SEQ = ("seq_0", "seq_1", "seq_2")


NEG_FILL = -1e30
NORM_EPS = 1e-06


def from_partner(block, axis, distance):
    count = lax.axis_size(axis)
    route = []
    for low in range(count):
        high = low | 1 << distance
        if high != low and high < count:
            route += [(low, high), (high, low)]
    return lax.ppermute(block, axis, route)


def copy_for_each(shard, axis):
    copies = jnp.broadcast_to(shard, (lax.axis_size(axis), *shard.shape))
    return lax.all_to_all(copies, axis, split_axis=0, concat_axis=0, tiled=True)


def in_order(blocks, dim):
    shape = list(blocks.shape[1:])
    shape[dim] *= blocks.shape[0]
    return jnp.moveaxis(blocks, 0, dim).reshape(shape)


def gather_axes(shard, axes, dim):
    far, near = axes
    initial = copy_for_each(shard, far)
    blocks = jnp.swapaxes(copy_for_each(initial, near), 0, 1)
    return in_order(blocks.reshape(-1, *shard.shape), dim)


def in_one_piece(arrays, axis, dim, along):
    widths = [a.shape[along] for a in arrays]
    both = jnp.concatenate(arrays, axis=along)
    out = gather_axes(both, axis, dim)
    return tuple(jnp.split(out, [sum(widths[:k]) for k in range(1, len(widths))], axis=along))


def of_everyone(shard, axis):
    return copy_for_each(shard, axis).sum(axis=0)


def in_blocks(shard, dim, size):
    before, after = (shard.shape[:dim], shard.shape[dim + 1 :])
    return jnp.moveaxis(shard.reshape(*before, size, -1, *after), dim, 0)


def sent_and_summed(shard, axis, dim):
    size = lax.axis_size(axis)
    blocks = lax.all_to_all(in_blocks(shard, dim, size), axis, 0, 0, tiled=True)
    return jnp.sum(blocks.astype(jnp.float32), axis=0)


def filled_up(lines, size):
    spare = -lines.shape[0] % size
    if not spare:
        return lines
    return jnp.concatenate([lines, jnp.zeros((spare, *lines.shape[1:]), lines.dtype)])


def collect(shard, axis, dim):
    blocks = copy_for_each(shard, axis)
    return in_order(blocks, dim)


def nested_sum(shard, axes):
    lines = shard.reshape(-1, shard.shape[-1])
    own = sent_and_summed(filled_up(lines, lax.axis_size(axes)), axes, 0)
    whole = collect(own.astype(jnp.bfloat16), axes, 0)
    return whole[: len(lines)].reshape(shard.shape).astype(jnp.float32)


def dot_rows(left, right):
    return lax.dot_general(
        left, right, (((1,), (1,)), ((), ())), preferred_element_type=jnp.float32
    )


def dot_columns(left, right):
    return lax.dot_general(
        left, right, (((0,), (0,)), ((), ())), preferred_element_type=jnp.float32
    )


def per_device(queries, keys, values, key_keep, global_positions, gain, cotangent):
    rows_dev = queries.shape[0]
    kv_heads = keys.shape[1] // HD
    q_heads = queries.shape[1] // HD
    group_size = QH // KVH
    scaling = HD ** (-0.5)
    global_count = global_positions.shape[0]
    bit_count = lax.axis_size(SEQ).bit_length() - 1
    offset_rows = lax.axis_index(SEQ) * rows_dev
    bit_order = list(range(bit_count))
    positions = jnp.arange(rows_dev, dtype=jnp.int32)
    key_blocks = [keys]
    value_blocks = [values]
    masks = [(key_keep[None, :] == 1) | (positions[:, None] == positions[None, :])]
    for bit_number in bit_order:
        partner_keys, partner_values, partner_keep = from_partner(
            (keys, values, key_keep), SEQ, bit_number
        )
        key_blocks.append(partner_keys)
        value_blocks.append(partner_values)
        masks.append(jnp.broadcast_to(partner_keep[None, :] == 1, (rows_dev, rows_dev)))
    selector = (global_positions[:, None] - offset_rows == positions[None, :]).astype(jnp.float32)
    piece = (
        *in_one_piece((keys, values), (("seq_0", "seq_1"), "seq_2"), 0, 1),
        gather_axes(key_keep, (("seq_0", "seq_1"), "seq_2"), 0),
    )
    count = piece[0].shape[0]
    chooser = (global_positions[:, None] == jnp.arange(count, dtype=jnp.int32)[None, :]).astype(
        jnp.float32
    )
    chooser_bf = chooser.astype(jnp.bfloat16)
    picked = (
        jnp.dot(chooser_bf, piece[0], preferred_element_type=jnp.float32),
        jnp.dot(chooser_bf, piece[1], preferred_element_type=jnp.float32),
        jnp.dot(chooser, piece[2].astype(jnp.float32), precision=lax.Precision.HIGHEST),
    )
    key_blocks.append(picked[0].astype(jnp.bfloat16))
    value_blocks.append(picked[1].astype(jnp.bfloat16))
    masks.append(jnp.broadcast_to(picked[2][None, :] > 0.5, (rows_dev, global_count)))
    all_keys = jnp.concatenate(key_blocks, 0)
    all_values = jnp.concatenate(value_blocks, 0)
    visible = jnp.concatenate(masks, 1)
    slots = all_keys.shape[0]
    key_stack = all_keys.reshape(slots, kv_heads, HD).transpose(1, 0, 2)
    value_stack = all_values.reshape(slots, kv_heads, HD).transpose(1, 0, 2)
    query_stack = queries.reshape(rows_dev, q_heads, HD).transpose(1, 0, 2)
    heads_order = jnp.arange(q_heads, dtype=jnp.int32)

    def head_scores(head_number, query_rows):
        owner = head_number // group_size
        key_rows = lax.dynamic_index_in_dim(key_stack, owner, 0, keepdims=False)
        value_rows = lax.dynamic_index_in_dim(value_stack, owner, 0, keepdims=False)
        scores = dot_rows(query_rows, key_rows) * scaling
        return (jnp.where(visible, scores, NEG_FILL), owner, key_rows, value_rows)

    def forward_head(operands):
        head_number, query_rows = operands
        scores, owner, key_rows, value_rows = head_scores(head_number, query_rows)
        peak = jnp.max(scores, -1, keepdims=True)
        expo = jnp.exp(scores - peak)
        total = jnp.sum(expo, -1, keepdims=True)
        mixed = (
            jnp.dot(expo.astype(jnp.bfloat16), value_rows, preferred_element_type=jnp.float32)
            / total
        )
        return (mixed, peak[:, 0], total[:, 0])

    attended, peaks, totals = lax.map(forward_head, (heads_order, query_stack))
    attn = attended.transpose(1, 0, 2).reshape(rows_dev, q_heads * HD)
    feature_count = QH * HD
    squares = of_everyone(jnp.sum(attn * attn, -1), "head")
    inverse = lax.rsqrt(squares / feature_count + NORM_EPS)
    gain_wide = gain.astype(jnp.float32)
    normed = (attn * inverse[:, None] * gain_wide).astype(jnp.bfloat16)
    upstream = cotangent.astype(jnp.float32) * gain_wide
    crossed = of_everyone(jnp.sum(upstream * attn, -1), "head")
    d_attn = inverse[:, None] * upstream - attn * (inverse**3 * crossed / feature_count)[:, None]
    d_stack = d_attn.reshape(rows_dev, q_heads, HD).transpose(1, 0, 2)
    d_stack_bf = d_stack.astype(jnp.bfloat16)

    def backward_head(carry, operands):
        head_number, query_rows, grad_rows, grad_rows_bf, attn_rows, peak, total = operands
        scores, owner, key_rows, value_rows = head_scores(head_number, query_rows)
        probs = jnp.exp(scores - peak[:, None]) / total[:, None]
        d_probs = dot_rows(grad_rows_bf, value_rows)
        diag_term = jnp.sum(grad_rows * attn_rows, -1, keepdims=True)
        d_scores = (probs * (d_probs - diag_term)).astype(jnp.bfloat16)
        d_query = jnp.dot(d_scores, key_rows, preferred_element_type=jnp.float32) * scaling
        d_key = dot_columns(d_scores, query_rows) * scaling
        d_value = dot_columns(probs.astype(jnp.bfloat16), grad_rows_bf)
        key_accum, value_accum = carry
        key_accum = lax.dynamic_update_index_in_dim(
            key_accum,
            lax.dynamic_index_in_dim(key_accum, owner, 0, keepdims=False) + d_key,
            owner,
            0,
        )
        value_accum = lax.dynamic_update_index_in_dim(
            value_accum,
            lax.dynamic_index_in_dim(value_accum, owner, 0, keepdims=False) + d_value,
            owner,
            0,
        )
        return ((key_accum, value_accum), d_query)

    zeros_stack = jnp.zeros((kv_heads, slots, HD), jnp.float32)
    (key_accum, value_accum), d_query_stack = lax.scan(
        backward_head,
        (zeros_stack, zeros_stack),
        (heads_order, query_stack, d_stack, d_stack_bf, attended, peaks, totals),
    )
    query_grad = (
        d_query_stack.transpose(1, 0, 2).reshape(rows_dev, q_heads * HD).astype(jnp.bfloat16)
    )
    key_slots = key_accum.transpose(1, 0, 2).reshape(slots, kv_heads * HD)
    value_slots = value_accum.transpose(1, 0, 2).reshape(slots, kv_heads * HD)
    key_running = key_slots[:rows_dev]
    value_running = value_slots[:rows_dev]
    for slot_number, bit_number in enumerate(bit_order):
        lower = rows_dev * (slot_number + 1)
        back_keys, back_values = (
            from_partner(
                key_slots[lower : lower + rows_dev].astype(jnp.bfloat16), SEQ, bit_number
            ).astype(jnp.float32),
            from_partner(
                value_slots[lower : lower + rows_dev].astype(jnp.bfloat16), SEQ, bit_number
            ).astype(jnp.float32),
        )
        key_running = key_running + back_keys
        value_running = value_running + back_values
    global_start = rows_dev * (len(bit_order) + 1)
    global_keys, global_values = (
        nested_sum(key_slots[global_start:].astype(jnp.bfloat16), SEQ),
        nested_sum(value_slots[global_start:].astype(jnp.bfloat16), SEQ),
    )
    key_running = key_running + lax.dot_general(
        selector, global_keys, (((0,), (0,)), ((), ())), precision=lax.Precision.HIGHEST
    )
    value_running = value_running + lax.dot_general(
        selector, global_values, (((0,), (0,)), ((), ())), precision=lax.Precision.HIGHEST
    )
    return (
        normed,
        query_grad,
        key_running.astype(jnp.bfloat16),
        value_running.astype(jnp.bfloat16),
    )


def solution(mesh):
    torus = Mesh(
        mesh.devices.reshape(4, 4, 2, mesh.shape["head"]), ("seq_0", "seq_1", "seq_2", "head")
    )
    in_specs = (
        P(SEQ, "head"),
        P(SEQ, "head"),
        P(SEQ, "head"),
        P(SEQ),
        P(),
        P("head"),
        P(SEQ, "head"),
    )
    out_specs = (P(SEQ, "head"), P(SEQ, "head"), P(SEQ, "head"), P(SEQ, "head"))
    return jax.shard_map(
        per_device, mesh=torus, in_specs=in_specs, out_specs=out_specs, check_vma=False
    )
```

profile of v0, /device:TPU:1, one launch (start us, length us, event | category | flops | bytes accessed | tf_op | source)
XLA Modules:
  0.0 288.8 jit_solution(4036528123840515713)
XLA Ops:
  0.7 3.3 %collective-permute-start = (bf16[256,128]{1,0:T(8,128)(2,1)}, bf16[256,128]{1,0:T(8,128)(2,1)}, u32[]{:S(2)}, u32[]{:S(2)}) collective-permute-start(bf16[256,128]{1,0:T(8,128)(2,1)} %param.12), channel_id=1, source_target_pairs={{0,8},{8,0},{16,24},{24,16},{32,40},{40,32},{48,56},{56,48},{64,72... | collective-permute-start | bytes 196616 | tf_op jit(solution)/shard_map/ppermute | solution.py:24
  3.9 2.9 %collective-permute-start.2 = (bf16[256,128]{1,0:T(8,128)(2,1)}, bf16[256,128]{1,0:T(8,128)(2,1)}, u32[]{:S(2)}, u32[]{:S(2)}) collective-permute-start(bf16[256,128]{1,0:T(8,128)(2,1)} %param.12), channel_id=1, source_target_pairs={{0,32},{32,0},{8,40},{40,8},{16,48},{48,16},{24,56},{56,24},{64,96... | collective-permute-start | bytes 196616 | tf_op jit(solution)/shard_map/ppermute | solution.py:24
  10.3 3.8 %all-to-all-start.2 = ((s32[16,1,256]{2,1,0:T(1,128)}), s32[16,1,256]{2,1,0:T(1,128)S(1)}, u32[]{:S(2)}, u32[]{:S(2)}) async-start(s32[16,1,256]{2,1,0:T(1,128)} %broadcast_in_dim.123), calls=%async_computation.2 | async-start | bytes 32768 | tf_op jit(solution)/shard_map/all_to_all | solution.py:29
  23.6 4.1 %all-to-all-start.3 = ((s32[2,16,256]{2,1,0:T(8,128)}), s32[2,16,256]{2,1,0:T(8,128)S(1)}, u32[]{:S(2)}, u32[]{:S(2)}) async-start(s32[2,16,256]{2,1,0:T(8,128)} %broadcast_in_dim.124), calls=%async_computation.3 | async-start | bytes 65536 | tf_op jit(solution)/shard_map/all_to_all | solution.py:29
  31.3 5.0 %all-to-all-start = ((bf16[16,256,256]{2,1,0:T(8,128)(2,1)}), bf16[16,256,256]{2,1,0:T(8,128)(2,1)}, u32[]{:S(2)}, u32[]{:S(2)}) async-start(bf16[16,256,256]{2,1,0:T(8,128)(2,1)} %broadcast_in_dim.116), calls=%async_computation | async-start | bytes 4194304 | tf_op jit(solution)/shard_map/all_to_all | solution.py:29
  37.8 12.3 %collective-permute-done.8 = s32[256]{0:T(256)S(1)} collective-permute-done((s32[256]{0:T(256)S(1)}, s32[256]{0:T(256)S(1)}, u32[]{:S(2)}, u32[]{:S(2)}) %collective-permute-start.8) | collective-permute-done | bytes 1056 | tf_op jit(solution)/shard_map/ppermute | solution.py:24
  52.4 3.1 %collective-permute-done.9 = s32[256]{0:T(256)S(1)} collective-permute-done((s32[256]{0:T(256)S(1)}, s32[256]{0:T(256)S(1)}, u32[]{:S(2)}, u32[]{:S(2)}) %collective-permute-start.9) | collective-permute-done | bytes 1056 | tf_op jit(solution)/shard_map/ppermute | solution.py:24
  57.1 5.7 %fusion.59 = f32[384]{0:T(512)S(1)} fusion(f32[8192,1]{0,1:T(1,128)S(1)} %reshape.112, s32[384]{0:T(512)S(1)} %copy-done.5), kind=kOutput, calls=%fused_computation.63 | convolution fusion | flops 40894464 | bytes 35840 | tf_op jit(solution)/shard_map/dot_general | solution.py:132
  63.1 6.5 %collective-permute-start.10 = (bf16[256,128]{1,0:T(8,128)(2,1)S(1)}, bf16[256,128]{1,0:T(8,128)(2,1)S(1)}, u32[]{:S(2)}, u32[]{:S(2)}) collective-permute-start(bf16[256,128]{1,0:T(8,128)(2,1)S(1)} %copy-done.3), channel_id=1, source_target_pairs={{0,8},{8,0},{16,24},{24,16},{32,40},{40,32},{48,56},{56,48},{64,72... | collective-permute-start | bytes 196616 | tf_op jit(solution)/shard_map/ppermute | solution.py:24
  77.7 9.3 %collective-permute-done.12 = bf16[256,128]{1,0:T(8,128)(2,1)S(1)} collective-permute-done((bf16[256,128]{1,0:T(8,128)(2,1)S(1)}, bf16[256,128]{1,0:T(8,128)(2,1)S(1)}, u32[]{:S(2)}, u32[]{:S(2)}) %collective-permute-start.12) | collective-permute-done | bytes 65568 | tf_op jit(solution)/shard_map/ppermute | solution.py:24
  89.7 8.8 %all_to_all.56 = bf16[2,16,256,256]{3,2,1,0:T(8,128)(2,1)S(1)} all-to-all(bf16[2,16,256,256]{3,2,1,0:T(8,128)(2,1)S(1)} %broadcast_in_dim.117), channel_id=1, replica_groups=mesh['seq_0'=4,'seq_1'=4,'seq_2'=2,'head'=8] {'seq_2'}, dimensions={0} | all-to-all | bytes 8388608 | tf_op jit(solution)/shard_map/all_to_all | solution.py:29
  102.9 32.9 %while.32 = (s32[]{:T(128)}, f32[8,256,128]{2,1,0:T(8,128)S(1)}, f32[8,256]{1,0:T(8,128)}, f32[8,256]{1,0:T(8,128)}, bf16[8,256,128]{2,1,0:T(8,128)(2,1)S(1)}, /...) while((s32[]{:T(128)}, f32[8,256,128]{2,1,0:T(8,128)S(1)}, ...), condition=%wide.region_3.4_spmd.clone, body=%wide.region_0.3_spmd.sunk.clone | while | flops 255131136 | bytes 7578725 | solution.py:165
  138.0 9.5 %all-to-all-start.5 = ((f32[8,1,256]{2,1,0:T(1,128)}), f32[8,1,256]{2,1,0:T(1,128)S(1)}, u32[]{:S(2)}, u32[]{:S(2)}) async-start(f32[8,1,256]{2,1,0:T(1,128)} %broadcast_in_dim.128), calls=%async_computation.5 | async-start | bytes 16384 | tf_op jit(solution)/shard_map/all_to_all | solution.py:29
  147.6 8.8 %all-to-all-done.5 = f32[8,1,256]{2,1,0:T(1,128)S(1)} async-done(((f32[8,1,256]{2,1,0:T(1,128)}), f32[8,1,256]{2,1,0:T(1,128)S(1)}, u32[]{:S(2)}, u32[]{:S(2)}) %all-to-all-start.5) | async-done | bytes 8224 | tf_op jit(solution)/shard_map/all_to_all | solution.py:29
  157.0 3.3 %all-to-all-start.4 = ((f32[8,1,256]{2,1,0:T(1,128)}), f32[8,1,256]{2,1,0:T(1,128)S(1)}, u32[]{:S(2)}, u32[]{:S(2)}) async-start(f32[8,1,256]{2,1,0:T(1,128)} %broadcast_in_dim.126), calls=%async_computation.4 | async-start | bytes 16384 | tf_op jit(solution)/shard_map/all_to_all | solution.py:29
  162.2 7.0 %all-to-all-done.4 = f32[8,1,256]{2,1,0:T(1,128)S(1)} async-done(((f32[8,1,256]{2,1,0:T(1,128)}), f32[8,1,256]{2,1,0:T(1,128)S(1)}, u32[]{:S(2)}, u32[]{:S(2)}) %all-to-all-start.4) | async-done | bytes 8224 | tf_op jit(solution)/shard_map/all_to_all | solution.py:29
  172.7 55.9 %while.33 = (s32[]{:T(128)}, f32[1,1920,128]{2,1,0:T(8,128)S(1)}, f32[1,1920,128]{2,1,0:T(8,128)S(1)}, bf16[8,256,128]{2,1,0:T(8,128)(2,1)}, bf16[8,256,128]{2,1...) while((s32[]{:T(128)}, f32[1,1920,128]{2,1,0:T(8,128)S(1)}, ...), condition=%wide.region_10.11_spmd.clone, body=%wide.region_8.10_spmd.sunk.clone | while | flops 633913088 | bytes 15410829 | solution.py:204
  229.4 7.5 %all-to-all-start.8 = ((bf16[32,12,128]{2,1,0:T(8,128)(2,1)}), bf16[32,12,128]{2,1,0:T(8,128)(2,1)S(1)}, u32[]{:S(2)}, u32[]{:S(2)}) async-start(bf16[32,12,128]{2,1,0:T(8,128)(2,1)} %convert_element_type.183), calls=%async_computation.8 | async-start | bytes 262144 | tf_op jit(solution)/shard_map/all_to_all | solution.py:63
  246.0 4.6 %all-to-all-start.6 = ((bf16[32,12,128]{2,1,0:T(8,128)(2,1)}), bf16[32,12,128]{2,1,0:T(8,128)(2,1)S(1)}, u32[]{:S(2)}, u32[]{:S(2)}) async-start(bf16[32,12,128]{2,1,0:T(8,128)(2,1)} %convert_element_type.171), calls=%async_computation.6 | async-start | bytes 262144 | tf_op jit(solution)/shard_map/all_to_all | solution.py:63
  251.5 7.9 %all-to-all-done.6 = bf16[32,12,128]{2,1,0:T(8,128)(2,1)S(1)} async-done(((bf16[32,12,128]{2,1,0:T(8,128)(2,1)}), bf16[32,12,128]{2,1,0:T(8,128)(2,1)S(1)}, u32[]{:S(2)}, u32[]{:S(2)}) %all-to-all-start.6) | async-done | bytes 98336 | tf_op jit(solution)/shard_map/all_to_all | solution.py:63
  260.1 3.9 %all-to-all-start.9 = ((bf16[32,12,128]{2,1,0:T(8,128)(2,1)}), bf16[32,12,128]{2,1,0:T(8,128)(2,1)S(1)}, u32[]{:S(2)}, u32[]{:S(2)}) async-start(bf16[32,12,128]{2,1,0:T(8,128)(2,1)} %broadcast_in_dim.130), calls=%async_computation.9 | async-start | bytes 262144 | tf_op jit(solution)/shard_map/all_to_all | solution.py:29
  264.7 8.1 %all-to-all-done.9 = bf16[32,12,128]{2,1,0:T(8,128)(2,1)S(1)} async-done(((bf16[32,12,128]{2,1,0:T(8,128)(2,1)}), bf16[32,12,128]{2,1,0:T(8,128)(2,1)S(1)}, u32[]{:S(2)}, u32[]{:S(2)}) %all-to-all-start.9) | async-done | bytes 98336 | tf_op jit(solution)/shard_map/all_to_all | solution.py:29
  273.4 3.9 %all-to-all-start.7 = ((bf16[32,12,128]{2,1,0:T(8,128)(2,1)}), bf16[32,12,128]{2,1,0:T(8,128)(2,1)S(1)}, u32[]{:S(2)}, u32[]{:S(2)}) async-start(bf16[32,12,128]{2,1,0:T(8,128)(2,1)} %broadcast_in_dim.129), calls=%async_computation.7 | async-start | bytes 262144 | tf_op jit(solution)/shard_map/all_to_all | solution.py:29
  282.6 2.5 collective-permute-start.19
  (237 shorter events, 155.3 us)
Async XLA Ops:
  0.7 62.4 %collective-permute-start = (bf16[256,128]{1,0:T(8,128)(2,1)}, bf16[256,128]{1,0:T(8,128)(2,1)}, u32[]{:S(2)}, u32[]{:S(2)}) collective-permute-start(bf16[256,128]{1,0:T(8,128)(2,1)} %param.12), channel_id=1, source_target_pairs={{0,8},{8,0},{16,24},{24,16},{32,40},{40,32},{48,56},{56,48},{64,72... | collective-permute-start | bytes 196616 | tf_op jit(solution)/shard_map/ppermute | solution.py:24
  3.9 66.5 %collective-permute-start.1 = (bf16[256,128]{1,0:T(8,128)(2,1)}, bf16[256,128]{1,0:T(8,128)(2,1)}, u32[]{:S(2)}, u32[]{:S(2)}) collective-permute-start(bf16[256,128]{1,0:T(8,128)(2,1)} %param.12), channel_id=1, source_target_pairs={{0,16},{16,0},{8,24},{24,8},{32,48},{48,32},{40,56},{56,40},{64,80... | collective-permute-start | bytes 196616 | tf_op jit(solution)/shard_map/ppermute | solution.py:24
  3.9 67.5 %collective-permute-start.2 = (bf16[256,128]{1,0:T(8,128)(2,1)}, bf16[256,128]{1,0:T(8,128)(2,1)}, u32[]{:S(2)}, u32[]{:S(2)}) collective-permute-start(bf16[256,128]{1,0:T(8,128)(2,1)} %param.12), channel_id=1, source_target_pairs={{0,32},{32,0},{8,40},{40,8},{16,48},{48,16},{24,56},{56,24},{64,96... | collective-permute-start | bytes 196616 | tf_op jit(solution)/shard_map/ppermute | solution.py:24
  6.9 66.2 %collective-permute-start.3 = (bf16[256,128]{1,0:T(8,128)(2,1)}, bf16[256,128]{1,0:T(8,128)(2,1)}, u32[]{:S(2)}, u32[]{:S(2)}) collective-permute-start(bf16[256,128]{1,0:T(8,128)(2,1)} %param.12), channel_id=1, source_target_pairs={{0,64},{64,0},{8,72},{72,8},{16,80},{80,16},{24,88},{88,24},{32,96... | collective-permute-start | bytes 196616 | tf_op jit(solution)/shard_map/ppermute | solution.py:24
  8.1 13.5 %collective-permute-start.5 = (s32[256]{0:T(256)}, s32[256]{0:T(256)S(1)}, u32[]{:S(2)}, u32[]{:S(2)}) collective-permute-start(s32[256]{0:T(256)} %param.14), channel_id=1, source_target_pairs={{0,8},{8,0},{16,24},{24,16},{32,40},{40,32},{48,56},{56,48},{64,72... | collective-permute-start | bytes 3080 | tf_op jit(solution)/shard_map/ppermute | solution.py:24
  10.3 12.7 %all-to-all-start.2 = ((s32[16,1,256]{2,1,0:T(1,128)}), s32[16,1,256]{2,1,0:T(1,128)S(1)}, u32[]{:S(2)}, u32[]{:S(2)}) async-start(s32[16,1,256]{2,1,0:T(1,128)} %broadcast_in_dim.123), calls=%async_computation.2 | async-start | bytes 32768 | tf_op jit(solution)/shard_map/all_to_all | solution.py:29
  31.3 56.3 %all-to-all-start = ((bf16[16,256,256]{2,1,0:T(8,128)(2,1)}), bf16[16,256,256]{2,1,0:T(8,128)(2,1)}, u32[]{:S(2)}, u32[]{:S(2)}) async-start(bf16[16,256,256]{2,1,0:T(8,128)(2,1)} %broadcast_in_dim.116), calls=%async_computation | async-start | bytes 4194304 | tf_op jit(solution)/shard_map/all_to_all | solution.py:29
  36.4 13.7 %collective-permute-start.8 = (s32[256]{0:T(256)S(1)}, s32[256]{0:T(256)S(1)}, u32[]{:S(2)}, u32[]{:S(2)}) collective-permute-start(s32[256]{0:T(256)S(1)} %copy-done.7), channel_id=1, source_target_pairs={{0,64},{64,0},{8,72},{72,8},{16,80},{80,16},{24,88},{88,24},{32,96... | collective-permute-start | bytes 3080 | tf_op jit(solution)/shard_map/ppermute | solution.py:24
  55.6 20.3 %collective-permute-start.4 = (bf16[256,128]{1,0:T(8,128)(2,1)}, bf16[256,128]{1,0:T(8,128)(2,1)}, u32[]{:S(2)}, u32[]{:S(2)}) collective-permute-start(bf16[256,128]{1,0:T(8,128)(2,1)} %param.12), channel_id=1, source_target_pairs={{0,128},{128,0},{8,136},{136,8},{16,144},{144,16},{24,152},{152,24... | collective-permute-start | bytes 196616 | tf_op jit(solution)/shard_map/ppermute | solution.py:24
  63.1 14.6 %collective-permute-start.10 = (bf16[256,128]{1,0:T(8,128)(2,1)S(1)}, bf16[256,128]{1,0:T(8,128)(2,1)S(1)}, u32[]{:S(2)}, u32[]{:S(2)}) collective-permute-start(bf16[256,128]{1,0:T(8,128)(2,1)S(1)} %copy-done.3), channel_id=1, source_target_pairs={{0,8},{8,0},{16,24},{24,16},{32,40},{40,32},{48,56},{56,48},{64,72... | collective-permute-start | bytes 196616 | tf_op jit(solution)/shard_map/ppermute | solution.py:24
  71.4 15.6 %collective-permute-start.12 = (bf16[256,128]{1,0:T(8,128)(2,1)S(1)}, bf16[256,128]{1,0:T(8,128)(2,1)S(1)}, u32[]{:S(2)}, u32[]{:S(2)}) collective-permute-start(bf16[256,128]{1,0:T(8,128)(2,1)S(1)} %copy-done.3), channel_id=1, source_target_pairs={{0,32},{32,0},{8,40},{40,8},{16,48},{48,16},{24,56},{56,24},{64,96... | collective-permute-start | bytes 196616 | tf_op jit(solution)/shard_map/ppermute | solution.py:24
  73.1 14.0 %collective-permute-start.13 = (bf16[256,128]{1,0:T(8,128)(2,1)S(1)}, bf16[256,128]{1,0:T(8,128)(2,1)S(1)}, u32[]{:S(2)}, u32[]{:S(2)}) collective-permute-start(bf16[256,128]{1,0:T(8,128)(2,1)S(1)} %copy-done.3), channel_id=1, source_target_pairs={{0,64},{64,0},{8,72},{72,8},{16,80},{80,16},{24,88},{88,24},{32,96... | collective-permute-start | bytes 196616 | tf_op jit(solution)/shard_map/ppermute | solution.py:24
  75.9 11.2 %collective-permute-start.14 = (bf16[256,128]{1,0:T(8,128)(2,1)S(1)}, bf16[256,128]{1,0:T(8,128)(2,1)S(1)}, u32[]{:S(2)}, u32[]{:S(2)}) collective-permute-start(bf16[256,128]{1,0:T(8,128)(2,1)S(1)} %copy-done.3), channel_id=1, source_target_pairs={{0,128},{128,0},{8,136},{136,8},{16,144},{144,16},{24,152},{152,24... | collective-permute-start | bytes 196616 | tf_op jit(solution)/shard_map/ppermute | solution.py:24
  138.0 18.4 %all-to-all-start.5 = ((f32[8,1,256]{2,1,0:T(1,128)}), f32[8,1,256]{2,1,0:T(1,128)S(1)}, u32[]{:S(2)}, u32[]{:S(2)}) async-start(f32[8,1,256]{2,1,0:T(1,128)} %broadcast_in_dim.128), calls=%async_computation.5 | async-start | bytes 16384 | tf_op jit(solution)/shard_map/all_to_all | solution.py:29
  157.0 12.2 %all-to-all-start.4 = ((f32[8,1,256]{2,1,0:T(1,128)}), f32[8,1,256]{2,1,0:T(1,128)S(1)}, u32[]{:S(2)}, u32[]{:S(2)}) async-start(f32[8,1,256]{2,1,0:T(1,128)} %broadcast_in_dim.126), calls=%async_computation.4 | async-start | bytes 16384 | tf_op jit(solution)/shard_map/all_to_all | solution.py:29
  229.4 16.6 %all-to-all-start.8 = ((bf16[32,12,128]{2,1,0:T(8,128)(2,1)}), bf16[32,12,128]{2,1,0:T(8,128)(2,1)S(1)}, u32[]{:S(2)}, u32[]{:S(2)}) async-start(bf16[32,12,128]{2,1,0:T(8,128)(2,1)} %convert_element_type.183), calls=%async_computation.8 | async-start | bytes 262144 | tf_op jit(solution)/shard_map/all_to_all | solution.py:63
  237.6 39.8 %collective-permute-start.20 = (bf16[256,128]{1,0:T(8,128)(2,1)}, bf16[256,128]{1,0:T(8,128)(2,1)S(1)}, u32[]{:S(2)}, u32[]{:S(2)}) collective-permute-start(bf16[256,128]{1,0:T(8,128)(2,1)} %get-tuple-element.305), channel_id=1, source_target_pairs={{0,8},{8,0},{16,24},{24,16},{32,40},{40,32},{48,56},{56,48},{64,72... | collective-permute-start | bytes 196616 | tf_op jit(solution)/shard_map/ppermute | solution.py:24
  237.9 40.0 %collective-permute-start.21 = (bf16[256,128]{1,0:T(8,128)(2,1)}, bf16[256,128]{1,0:T(8,128)(2,1)S(1)}, u32[]{:S(2)}, u32[]{:S(2)}) collective-permute-start(bf16[256,128]{1,0:T(8,128)(2,1)} %get-tuple-element.309), channel_id=1, source_target_pairs={{0,16},{16,0},{8,24},{24,8},{32,48},{48,32},{40,56},{56,40},{64,80... | collective-permute-start | bytes 196616 | tf_op jit(solution)/shard_map/ppermute | solution.py:24
  239.4 39.9 %collective-permute-start.22 = (bf16[256,128]{1,0:T(8,128)(2,1)}, bf16[256,128]{1,0:T(8,128)(2,1)S(1)}, u32[]{:S(2)}, u32[]{:S(2)}) collective-permute-start(bf16[256,128]{1,0:T(8,128)(2,1)} %get-tuple-element.308), channel_id=1, source_target_pairs={{0,32},{32,0},{8,40},{40,8},{16,48},{48,16},{24,56},{56,24},{64,96... | collective-permute-start | bytes 196616 | tf_op jit(solution)/shard_map/ppermute | solution.py:24
  241.5 39.9 %collective-permute-start.23 = (bf16[256,128]{1,0:T(8,128)(2,1)}, bf16[256,128]{1,0:T(8,128)(2,1)}, u32[]{:S(2)}, u32[]{:S(2)}) collective-permute-start(bf16[256,128]{1,0:T(8,128)(2,1)} %get-tuple-element.307), channel_id=1, source_target_pairs={{0,64},{64,0},{8,72},{72,8},{16,80},{80,16},{24,88},{88,24},{32,96... | collective-permute-start | bytes 196616 | tf_op jit(solution)/shard_map/ppermute | solution.py:24
  242.6 39.9 %collective-permute-start.24 = (bf16[256,128]{1,0:T(8,128)(2,1)S(1)}, bf16[256,128]{1,0:T(8,128)(2,1)}, u32[]{:S(2)}, u32[]{:S(2)}) collective-permute-start(bf16[256,128]{1,0:T(8,128)(2,1)S(1)} %get-tuple-element.306), channel_id=1, source_target_pairs={{0,128},{128,0},{8,136},{136,8},{16,144},{144,16},{24,152},{152,24... | collective-permute-start | bytes 196616 | tf_op jit(solution)/shard_map/ppermute | solution.py:24
  246.0 13.4 %all-to-all-start.6 = ((bf16[32,12,128]{2,1,0:T(8,128)(2,1)}), bf16[32,12,128]{2,1,0:T(8,128)(2,1)S(1)}, u32[]{:S(2)}, u32[]{:S(2)}) async-start(bf16[32,12,128]{2,1,0:T(8,128)(2,1)} %convert_element_type.171), calls=%async_computation.6 | async-start | bytes 262144 | tf_op jit(solution)/shard_map/all_to_all | solution.py:63
  260.1 12.7 %all-to-all-start.9 = ((bf16[32,12,128]{2,1,0:T(8,128)(2,1)}), bf16[32,12,128]{2,1,0:T(8,128)(2,1)S(1)}, u32[]{:S(2)}, u32[]{:S(2)}) async-start(bf16[32,12,128]{2,1,0:T(8,128)(2,1)} %broadcast_in_dim.130), calls=%async_computation.9 | async-start | bytes 262144 | tf_op jit(solution)/shard_map/all_to_all | solution.py:29
  273.4 13.5 %all-to-all-start.7 = ((bf16[32,12,128]{2,1,0:T(8,128)(2,1)}), bf16[32,12,128]{2,1,0:T(8,128)(2,1)S(1)}, u32[]{:S(2)}, u32[]{:S(2)}) async-start(bf16[32,12,128]{2,1,0:T(8,128)(2,1)} %broadcast_in_dim.129), calls=%async_computation.7 | async-start | bytes 262144 | tf_op jit(solution)/shard_map/all_to_all | solution.py:29
  (18 other events, 227.3 us)
where the time goes:
time: 292 us; the launch traced here: 289 us
  starting transfers between devices  88 us (30%)
  matrix products  61.8 us (21%)
  waiting for transfers between devices  58 us (20%)
  local copies, waits for them, and re-layouts  51.3 us (18%)
  other arithmetic  19.4 us (7%)
  blocking collectives  8.82 us (3%)
    ppermute x25, starting transfers between devices, from_partner(): return lax.ppermute(block, axis, route)  42.3 us
    all_to_all x7, starting transfers between devices, copy_for_each(): return lax.all_to_all(copies, axis, split_axis=0, concat_axis=0, tiled=True)  33.5 us
    ppermute x25, waiting for transfers between devices, from_partner(): return lax.ppermute(block, axis, route)  25.5 us
    all_to_all x7, waiting for transfers between devices, copy_for_each(): return lax.all_to_all(copies, axis, split_axis=0, concat_axis=0, tiled=True)  24.5 us
    dot_general x24, matrix products, dot_rows(): lax.dot_general(left, right, (((1,), (1,)), ((), ())), preferred_element_...  22.1 us
    dynamic_update_slice x16, local copies, waits for them, and re-layouts, per_device(): attended, peaks, totals = lax.map(forward_head, (heads_order, query_stack))  21 us
    dot_general x16, matrix products, dot_columns(): lax.dot_general(left, right, (((0,), (0,)), ((), ())), preferred_element_...  15 us
    all_to_all x2, starting transfers between devices, sent_and_summed(): blocks = lax.all_to_all(in_blocks(shard, dim, size), axis, 0, 0, tiled=True)  12.1 us
  transfers between devices with their start and end apart: 34, of which 10 were waited for; matrix products, arithmetic and copies ran while one was open for 10% of the time, Pallas kernels for 0%

commit v1 on v0

v1 whole, which is shorter than its diff:
```python
import functools

import jax
import jax.numpy as jnp
from jax import lax
from jax.experimental import pallas as pl
from jax.experimental.pallas import tpu as pltpu
from jax.sharding import Mesh
from jax.sharding import PartitionSpec as P

HD = 128
FEATURES = 8192
NEG_FILL = -1e30
NORM_EPS = 1e-06
SEQ = ("x", "z", "c")
HEAD = ("zh", "y")
SCALE = HD ** (-0.5)
SCALE2 = SCALE * 1.4426950408889634
F32 = jnp.float32
BF = jnp.bfloat16
H = 8
R = 256
G = 384
SLOTS = 6 * R + G

BLOCKS = [(R * i, R) for i in range(6)] + [(6 * R, G)]
GROUPS = [(0,), (1, 2), (4, 3), (5,), (6,)]


def nt(a, b):
    return lax.dot_general(a, b, (((1,), (1,)), ((), ())), preferred_element_type=F32)


def nn(a, b):
    return jnp.dot(a, b, preferred_element_type=F32)


def tn(a, b):
    return lax.dot_general(a, b, (((0,), (0,)), ((), ())), preferred_element_type=F32)


def wide(x, n):
    return jnp.concatenate([x] * (n // 128), 1)


def head_cols(h):
    return pl.ds(pl.multiple_of(h * HD, HD), HD)


def kernel(
    q_ref, k_ref, v_ref, keep_ref, gpos_ref, gain_ref, ct_ref,
    normed_ref, dq_ref, dk_ref, dv_ref,
    ks, vs, keeps, own_bias, expo, m_s, l_s, o_s, f_s, attn, d_attn, diag, dqs, dks, dvs,
    ga, gc, hb, gx, pb, gz, hfull, full,
    fl, flc, flx, flz,
    st, st_in, grad_out, grad_in,
    kv_send, kv_recv, g_send, g_recv, f_send, f_recv, st_send, st_recv, gr_send, gr_recv,
):
    x, z, c = lax.axis_index("x"), lax.axis_index("z"), lax.axis_index("c")
    zh, y = lax.axis_index("zh"), lax.axis_index("y")
    x_peers = [lax.rem(x + o, 4) for o in (1, 2, 3)]
    z_peers = [lax.rem(z + o, 4) for o in (1, 2, 3)]
    head_peers = [
        {"zh": lax.rem(zh + dz, 2), "y": lax.rem(y + dy, 4)}
        for dz in range(2)
        for dy in range(4)
        if dz or dy
    ]
    partners = [
        {"c": 1 - c},
        {"z": z + 1 - 2 * lax.rem(z, 2)},
        {"z": lax.rem(z + 2, 4)},
        {"x": x + 1 - 2 * lax.rem(x, 2)},
        {"x": lax.rem(x + 2, 4)},
    ]

    def remote(src, dst, send, recv, device):
        return pltpu.make_async_remote_copy(
            src_ref=src, dst_ref=dst, send_sem=send, recv_sem=recv,
            device_id=device, device_id_type=pl.DeviceIdType.MESH,
        )

    barrier = pltpu.get_barrier_semaphore()
    everyone = [{"c": 1 - c}] + [{"x": p} for p in x_peers] + [{"z": p} for p in z_peers] + head_peers
    for peer in everyone:
        pl.semaphore_signal(barrier, inc=1, device_id=peer, device_id_type=pl.DeviceIdType.MESH)

    offset = (x * 8 + z * 2 + c) * R
    rows = lax.broadcasted_iota(jnp.int32, (R, G), 0)
    chosen = (jnp.broadcast_to(gpos_ref[...], (R, G)) - offset == rows).astype(F32).astype(BF)
    own_kv = jnp.concatenate([k_ref[...], v_ref[...]], 1)
    ga[0] = tn(chosen, own_kv).astype(BF).reshape(2, G // 2, 2 * HD)
    keep_rows = jnp.broadcast_to(keep_ref[...], (8, R)).astype(F32).astype(BF)
    fl[0] = nn(keep_rows, chosen)
    eye = lax.broadcasted_iota(jnp.int32, (R, R), 0) == lax.broadcasted_iota(jnp.int32, (R, R), 1)
    row_bias = jnp.where(jnp.broadcast_to(keep_ref[...], (R, R)) == 1, 0.0, NEG_FILL)
    own_bias[...] = jnp.where(eye, 0.0, row_bias)
    ks[0:R] = k_ref[...]
    vs[0:R] = v_ref[...]

    pl.semaphore_wait(barrier, len(everyone))

    def kv_copies(b):
        lower = R * (b + 1)
        return [
            remote(k_ref, ks.at[pl.ds(lower, R)], kv_send.at[0, b], kv_recv.at[0, b], partners[b]),
            remote(v_ref, vs.at[pl.ds(lower, R)], kv_send.at[1, b], kv_recv.at[1, b], partners[b]),
            remote(keep_ref, keeps.at[b], kv_send.at[2, b], kv_recv.at[2, b], partners[b]),
        ]

    def started(copies):
        for copy in copies:
            copy.start()
        return copies

    def waited(copies):
        for copy in copies:
            copy.wait()

    def core_stage(t):
        return remote(ga.at[t, 1 - c], gc.at[t], g_send.at[t, 0], g_recv.at[t, 0], {"c": 1 - c})

    def x_stage(t):
        return [
            remote(hb.at[t, p], gx.at[t, i], g_send.at[t, 1 + i], g_recv.at[t, 1 + i], {"x": p})
            for i, p in enumerate(x_peers)
        ]

    def z_stage(t):
        return [
            remote(pb.at[t], gz.at[t, i], g_send.at[t, 4 + i], g_recv.at[t, 4 + i], {"z": p})
            for i, p in enumerate(z_peers)
        ]

    def x_back(t):
        return [
            remote(hfull.at[t, x], hfull.at[t, x], g_send.at[t, 7 + i], g_recv.at[t, 7 + i], {"x": p})
            for i, p in enumerate(x_peers)
        ]

    def core_back(t):
        return remote(full.at[t, c], full.at[t, c], g_send.at[t, 10], g_recv.at[t, 10], {"c": 1 - c})

    def add_core(t):
        total = ga[t, c].astype(F32) + gc[t].astype(F32)
        hb[t] = total.astype(BF).reshape(4, G // 8, 2 * HD)

    def add_x(t):
        total = hb[t, x].astype(F32)
        for i in range(3):
            total = total + gx[t, i].astype(F32)
        pb[t] = total.astype(BF)

    def add_z(t):
        total = pb[t].astype(F32)
        for i in range(3):
            total = total + gz[t, i].astype(F32)
        hfull[t, x] = total.astype(BF)

    def flag_stage(s):
        if s == 0:
            return [remote(fl.at[0], flc, f_send.at[0], f_recv.at[0], {"c": 1 - c})]
        peers = [{"x": p} for p in x_peers] if s == 1 else [{"z": p} for p in z_peers]
        into = flx if s == 1 else flz
        base = 1 if s == 1 else 4
        return [
            remote(fl.at[s], into.at[i], f_send.at[base + i], f_recv.at[base + i], p)
            for i, p in enumerate(peers)
        ]

    def forward_group(g, bias):
        blocks = [BLOCKS[b] for b in GROUPS[g]]

        def body(h, carry):
            q = q_ref[:, head_cols(h)]
            parts, top = [], None
            for lower, size in blocks:
                s = nt(q, ks[lower : lower + size])
                s = s + (own_bias[...] if lower == 0 else bias[lower])
                parts.append(s)
                for j in range(0, size, 128):
                    piece = s[:, j : j + 128]
                    top = piece if top is None else jnp.maximum(top, piece)
            peak = jnp.broadcast_to(jnp.max(top, 1, keepdims=True), (R, 128)) * SCALE2
            mixed, total = None, None
            for (lower, size), s in zip(blocks, parts):
                e = jnp.exp2(s * SCALE2 - wide(peak, size))
                for j in range(0, size, 128):
                    piece = e[:, j : j + 128]
                    total = piece if total is None else total + piece
                e_bf = e.astype(BF)
                expo[h, :, lower : lower + size] = e_bf
                term = nn(e_bf, vs[lower : lower + size])
                mixed = term if mixed is None else mixed + term
            m_s[g, h] = peak
            l_s[g, h] = jnp.broadcast_to(jnp.sum(total, 1, keepdims=True), (R, 128))
            o_s[g, h] = mixed
            return carry

        lax.fori_loop(0, H, body, 0, unroll=2)

    def backward_group(g, first):
        blocks = [BLOCKS[b] for b in GROUPS[g]]

        def body(h, carry):
            q = q_ref[:, head_cols(h)]
            factor = f_s[g, h]
            grad = (d_attn[h] * factor).astype(BF)
            shift = diag[h] * factor
            q_t, grad_t = q.T, grad.T
            d_query = None
            for lower, size in blocks:
                e = expo[h, :, lower : lower + size]
                d_probs = nt(grad, vs[lower : lower + size])
                d_scores = (e.astype(F32) * (d_probs - wide(shift, size))).astype(BF)
                term = nn(d_scores, ks[lower : lower + size])
                d_query = term if d_query is None else d_query + term
                dks[:, lower : lower + size] += nn(q_t, d_scores)
                dvs[:, lower : lower + size] += nn(grad_t, e)
            if first:
                dqs[h] = d_query
            else:
                dqs[h] += d_query
            return carry

        lax.fori_loop(0, H, body, 0, unroll=2)

    def block_bias(*numbers):
        return {
            BLOCKS[b][0]: jnp.where(keeps[b - 1] == 1, 0.0, NEG_FILL).astype(F32) for b in numbers
        }

    core0 = started([core_stage(0)] + flag_stage(0))
    kv = {b: started(kv_copies(b)) for b in (0, 1)}
    waited(core0)
    add_core(0)
    fl[1] = fl[0] + flc[...]
    x0 = started(x_stage(0) + flag_stage(1))
    kv[3] = started(kv_copies(3))
    kv[4] = started(kv_copies(4))
    forward_group(0, {})
    waited(x0)
    add_x(0)
    fl[2] = fl[1] + flx[0] + flx[1] + flx[2]
    z0 = started(z_stage(0) + flag_stage(2))
    kv[2] = started(kv_copies(2))
    waited(kv[0])
    waited(kv[1])
    forward_group(1, block_bias(1, 2))
    waited(z0)
    add_z(0)
    global_keep = fl[2] + flz[0] + flz[1] + flz[2]
    xb0 = started(x_back(0))
    waited(kv[3])
    waited(kv[2])
    forward_group(2, block_bias(4, 3))
    waited(xb0)
    full[0, c] = hfull[0].reshape(G // 2, 2 * HD)
    cb0 = started([core_back(0)])
    waited(kv[4])
    forward_group(3, block_bias(5))
    waited(cb0)
    for half in range(2):
        lower = 6 * R + half * (G // 2)
        ks[lower : lower + G // 2] = full[0, half, :, :HD]
        vs[lower : lower + G // 2] = full[0, half, :, HD:]
    global_bias = jnp.where(global_keep[0:1] > 0.5, 0.0, NEG_FILL)
    forward_group(4, {6 * R: global_bias})

    def merge(h, carry):
        squares, crossed = carry
        peaks = [m_s[g, h] for g in range(len(GROUPS))]
        peak = functools.reduce(jnp.maximum, peaks)
        weights = [jnp.exp2(p - peak) for p in peaks]
        total = sum(w * l_s[g, h] for g, w in enumerate(weights))
        inv_total = 1.0 / total
        out = None
        for g, w in enumerate(weights):
            factor = w * inv_total
            f_s[g, h] = factor
            term = factor * o_s[g, h]
            out = term if out is None else out + term
        attn[h] = out
        up = ct_ref[:, head_cols(h)].astype(F32) * gain_ref[:, head_cols(h)].astype(F32)
        return (squares + out * out, crossed + up * out)

    zeros = jnp.zeros((R, HD), F32)
    squares, crossed = lax.fori_loop(0, H, merge, (zeros, zeros))
    rows8 = lax.broadcasted_iota(jnp.int32, (8, R), 0)
    squares_row = jnp.broadcast_to(jnp.sum(squares.T, 0, keepdims=True), (8, R))
    crossed_row = jnp.broadcast_to(jnp.sum(crossed.T, 0, keepdims=True), (8, R))
    st[...] = jnp.where(rows8 == 0, squares_row, crossed_row)
    stats = started(
        [
            remote(st, st_in.at[i], st_send.at[i], st_recv.at[i], peer)
            for i, peer in enumerate(head_peers)
        ]
    )
    dks[...] = jnp.zeros_like(dks)
    dvs[...] = jnp.zeros_like(dvs)
    waited(stats)
    both = st[...]
    for i in range(7):
        both = both + st_in[i]
    inverse = lax.rsqrt(both[0:1] / FEATURES + NORM_EPS)
    coef = inverse * inverse * inverse * both[1:2] / FEATURES
    inverse = jnp.broadcast_to(inverse, (HD, R)).T
    coef = jnp.broadcast_to(coef, (HD, R)).T

    def norm_grad(h, carry):
        out = attn[h]
        gain = gain_ref[:, head_cols(h)].astype(F32)
        up = ct_ref[:, head_cols(h)].astype(F32) * gain
        grad = inverse * up - out * coef
        d_attn[h] = grad
        diag[h] = jnp.broadcast_to(jnp.sum(grad * out, 1, keepdims=True), (R, HD))
        normed_ref[:, head_cols(h)] = (out * inverse * gain).astype(BF)
        return carry

    lax.fori_loop(0, H, norm_grad, 0)

    def send_grads(b):
        lower = R * (b + 1)
        grad_out[b, 0] = (dks[:, lower : lower + R] * SCALE).astype(BF)
        grad_out[b, 1] = dvs[:, lower : lower + R].astype(BF)
        return started(
            [remote(grad_out.at[b], grad_in.at[b], gr_send.at[b], gr_recv.at[b], partners[b])]
        )

    backward_group(4, True)
    d_global = jnp.concatenate([dks[:, 6 * R :] * SCALE, dvs[:, 6 * R :]], 0).T
    ga[1] = d_global.astype(BF).reshape(2, G // 2, 2 * HD)
    core1 = started([core_stage(1)])
    backward_group(3, False)
    waited(core1)
    add_core(1)
    x1 = started(x_stage(1))
    sent = send_grads(4)
    backward_group(2, False)
    waited(x1)
    add_x(1)
    z1 = started(z_stage(1))
    sent += send_grads(2) + send_grads(3)
    backward_group(1, False)
    waited(z1)
    add_z(1)
    xb1 = started(x_back(1))
    sent += send_grads(1) + send_grads(0)
    backward_group(0, False)

    def finish(h, carry):
        dq_ref[:, head_cols(h)] = (dqs[h] * SCALE).astype(BF)
        return carry

    lax.fori_loop(0, H, finish, 0)
    waited(xb1)
    full[1, c] = hfull[1].reshape(G // 2, 2 * HD)
    cb1 = started([core_back(1)])
    waited(sent)
    d_keys = dks[:, 0:R] * SCALE
    d_values = dvs[:, 0:R]
    for b in range(5):
        d_keys = d_keys + grad_in[b, 0].astype(F32)
        d_values = d_values + grad_in[b, 1].astype(F32)
    waited(cb1)
    back = nn(chosen, full[1].reshape(G, 2 * HD))
    dk_ref[...] = (d_keys.T + back[:, :HD]).astype(BF)
    dv_ref[...] = (d_values.T + back[:, HD:]).astype(BF)


def per_device(queries, keys, values, key_keep, global_positions, gain, cotangent):
    vmem = pl.BlockSpec(memory_space=pltpu.VMEM)
    ng = len(GROUPS)
    half, eighth, width = G // 2, G // 8, 2 * HD
    scratch = [
        pltpu.VMEM((SLOTS, HD), BF),
        pltpu.VMEM((SLOTS, HD), BF),
        pltpu.VMEM((5, 1, R), jnp.int32),
        pltpu.VMEM((R, R), F32),
        pltpu.VMEM((H, R, SLOTS), BF),
        *[pltpu.VMEM((ng, H, R, HD), F32)] * 4,
        *[pltpu.VMEM((H, R, HD), F32)] * 4,
        *[pltpu.VMEM((HD, SLOTS), F32)] * 2,
        pltpu.VMEM((2, 2, half, width), BF),
        pltpu.VMEM((2, half, width), BF),
        pltpu.VMEM((2, 4, eighth, width), BF),
        pltpu.VMEM((2, 3, eighth, width), BF),
        pltpu.VMEM((2, eighth, width), BF),
        pltpu.VMEM((2, 3, eighth, width), BF),
        pltpu.VMEM((2, 4, eighth, width), BF),
        pltpu.VMEM((2, 2, half, width), BF),
        pltpu.VMEM((3, 8, G), F32),
        pltpu.VMEM((8, G), F32),
        pltpu.VMEM((3, 8, G), F32),
        pltpu.VMEM((3, 8, G), F32),
        pltpu.VMEM((8, R), F32),
        pltpu.VMEM((7, 8, R), F32),
        pltpu.VMEM((5, 2, HD, R), BF),
        pltpu.VMEM((5, 2, HD, R), BF),
        *[pltpu.SemaphoreType.DMA((3, 5))] * 2,
        *[pltpu.SemaphoreType.DMA((2, 11))] * 2,
        *[pltpu.SemaphoreType.DMA((7,))] * 2,
        *[pltpu.SemaphoreType.DMA((7,))] * 2,
        *[pltpu.SemaphoreType.DMA((5,))] * 2,
    ]
    return pl.pallas_call(
        kernel,
        out_shape=(
            jax.ShapeDtypeStruct(queries.shape, BF),
            jax.ShapeDtypeStruct(queries.shape, BF),
            jax.ShapeDtypeStruct(keys.shape, BF),
            jax.ShapeDtypeStruct(values.shape, BF),
        ),
        in_specs=[vmem] * 7,
        out_specs=[vmem] * 4,
        scratch_shapes=scratch,
        compiler_params=pltpu.CompilerParams(
            collective_id=0, has_side_effects=True, vmem_limit_bytes=60 << 20
        ),
        name="butterfly",
    )(
        queries,
        keys,
        values,
        key_keep.reshape(1, R),
        global_positions.reshape(1, G),
        gain.reshape(1, -1),
        cotangent,
    )


def solution(mesh):
    torus = Mesh(mesh.devices.reshape(4, 4, 2, 2, 4), (*SEQ, *HEAD))
    in_specs = (
        P(SEQ, HEAD), P(SEQ, HEAD), P(SEQ, HEAD), P(SEQ), P(), P(HEAD), P(SEQ, HEAD),
    )
    return jax.shard_map(
        per_device,
        mesh=torus,
        in_specs=in_specs,
        out_specs=(P(SEQ, HEAD),) * 4,
        check_vma=False,
    )
```

time: 292 us -> 73.4 us (0.25)
  starting transfers between devices: 88 us -> 0 us
  Pallas kernels: 0 us -> 66.3 us
  matrix products: 61.8 us -> 0 us
  waiting for transfers between devices: 58 us -> 0 us
  local copies, waits for them, and re-layouts: 51.3 us -> 6.13 us
  other arithmetic: 19.4 us -> 0 us
  blocking collectives: 8.82 us -> 0 us
    pallas_call x0 -> x1, Pallas kernels: none -> 66.3 us  [per_device(): pl.pallas_call(kernel, out_shape=(jax.ShapeDtypeStruct(queries.shape, BF)...]
    dot_general x61 -> x0, matrix products: 61.8 us -> none  [the longest x24 22.1 us: dot_rows(): lax.dot_general(left, right, (((1,), (1,)), ((), ())), preferred_element_...]
    all_to_all x9 -> x0, starting transfers between devices: 45.6 us -> none  [the longest x7 33.5 us: copy_for_each(): return lax.all_to_all(copies, axis, split_axis=0, concat_axis=0, tiled=True)]
    ppermute x25 -> x0, starting transfers between devices: 42.3 us -> none  [from_partner(): return lax.ppermute(block, axis, route)]
    all_to_all x9 -> x0, waiting for transfers between devices: 32.5 us -> none  [the longest x7 24.5 us: copy_for_each(): return lax.all_to_all(copies, axis, split_axis=0, concat_axis=0, tiled=True)]
    ppermute x25 -> x0, waiting for transfers between devices: 25.5 us -> none  [from_partner(): return lax.ppermute(block, axis, route)]
    dynamic_update_slice x16 -> x0, local copies, waits for them, and re-layouts: 21 us -> none  [per_device(): attended, peaks, totals = lax.map(forward_head, (heads_order, query_stack))]
    reduce_sum x22 -> x0, other arithmetic: 14 us -> none  [the longest x8 8.68 us: backward_head(): diag_term = jnp.sum(grad_rows * attn_rows, -1, keepdims=True)]
  transfers between devices with their start and end apart: 34 -> 0, of which waited for: 10 -> 0; matrix products, arithmetic and copies ran while one was open for 10% -> 0% of each run, Pallas kernels for 0% -> 0%
where the time goes in v1:
time: 73.4 us; the launch traced here: 73.1 us
  Pallas kernels  66.3 us (90%)
  local copies, waits for them, and re-layouts  6.13 us (8%)
    pallas_call x1, Pallas kernels, per_device(): pl.pallas_call(kernel, out_shape=(jax.ShapeDtypeStruct(queries.shape, BF)...  66.3 us
    unnamed x12, local copies, waits for them, and re-layouts  4.29 us

profile of v1, /device:TPU:1, one launch (start us, length us, event | category | flops | bytes accessed | tf_op | source)
XLA Modules:
  0.0 73.1 jit_solution(3811354652399835283)
XLA Ops:
  0.6 0.0 copy-start.3
  0.6 1.3 %reshape.18.gpos_ref = s32[1,384]{1,0:T(1,128)} reshape(s32[384]{0:T(512)} %param.11) | data formatting | bytes 3072 | tf_op jit(solution)/shard_map/reshape | solution.py:426
  1.9 0.0 copy-done.3
  1.9 0.6 reshape.19.gain_ref
  2.5 66.3 %butterfly.1 = (bf16[256,1024]{1,0:T(8,128)(2,1)}, bf16[256,1024]{1,0:T(8,128)(2,1)}, bf16[256,128]{1,0:T(8,128)(2,1)}, bf16[256,128]{1,0:T(8,128)(2,1)}) custom-call(bf16[256,1024]{1,0:T(8,128)(2,1)} %q_ref.1, bf16[256,128]{1,0:T(8,128)(2,1)} %k_ref.1, bf16[256,128]{1,0:T(8,128)(2,1)} %v_ref.1, s32[1,256]{1,0:T(1,128)} %bitcast.1, ...), custom_call_target="tpu_custom_call" | custom-call | tf_op jit(solution)/shard_map/butterfly/pallas_call | solution.py:406
  68.8 0.0 copy-start
  68.8 1.9 %copy.15 = bf16[256,1024]{1,0:T(8,128)(2,1)} copy(bf16[256,1024]{1,0:T(8,128)(2,1)} %get-tuple-element.8) | data formatting | bytes 1048576
  70.8 0.0 copy-done
  70.8 0.0 copy-start.2
  70.8 0.8 %copy.16 = bf16[256,1024]{1,0:T(8,128)(2,1)} copy(bf16[256,1024]{1,0:T(8,128)(2,1)S(1)} %copy-done) | data formatting | bytes 1048576
  71.6 0.1 copy-done.2
  71.6 0.0 copy-start.1
  71.6 0.6 copy.17
  72.3 0.2 copy-done.1
  72.5 0.6 copy.18
Async XLA Ops:
  0.6 1.3 %copy-start.3 = (bf16[1024]{0:T(1024)(128)(2,1)S(1)}, bf16[1024]{0:T(1024)(128)(2,1)}, u32[]{:S(2)}) copy-start(bf16[1024]{0:T(1024)(128)(2,1)} %param.12) | copy-start | bytes 6148
  68.8 1.9 %copy-start = (bf16[256,1024]{1,0:T(8,128)(2,1)S(1)}, bf16[256,1024]{1,0:T(8,128)(2,1)}, u32[]{:S(2)}) copy-start(bf16[256,1024]{1,0:T(8,128)(2,1)} %get-tuple-element.9) | copy-start | bytes 1572868
  70.8 0.9 %copy-start.2 = (bf16[256,128]{1,0:T(8,128)(2,1)S(1)}, bf16[256,128]{1,0:T(8,128)(2,1)}, u32[]{:S(2)}) copy-start(bf16[256,128]{1,0:T(8,128)(2,1)} %get-tuple-element.10) | copy-start | bytes 196612
  71.6 0.9 %copy-start.1 = (bf16[256,128]{1,0:T(8,128)(2,1)S(1)}, bf16[256,128]{1,0:T(8,128)(2,1)}, u32[]{:S(2)}) copy-start(bf16[256,128]{1,0:T(8,128)(2,1)} %get-tuple-element.11) | copy-start | bytes 196612

commit v2 on v1

--- a/solution.py
+++ b/solution.py
@@ -48,13 +48,14 @@
 
 
 def kernel(
-    q_ref, k_ref, v_ref, keep_ref, gpos_ref, gain_ref, ct_ref,
+    q_hbm, k_hbm, v_hbm, keep_hbm, gpos_hbm, gain_hbm, ct_hbm,
     normed_ref, dq_ref, dk_ref, dv_ref,
+    q_ref, k_ref, v_ref, keep_ref, gpos_ref, gain_ref, ct_ref, in_sems,
     ks, vs, keeps, own_bias, expo, m_s, l_s, o_s, f_s, attn, d_attn, diag, dqs, dks, dvs,
     ga, gc, hb, gx, pb, gz, hfull, full,
     fl, flc, flx, flz,
-    st, st_in, grad_out, grad_in,
-    kv_send, kv_recv, g_send, g_recv, f_send, f_recv, st_send, st_recv, gr_send, gr_recv,
+    gains, squares, crossed, inverse, coef, st, st_in, grad_out, grad_in,
+    ring_sem, y_sem, kv_send, kv_recv, g_send, g_recv, f_send, f_recv, st_send, st_recv, gr_send, gr_recv,
 ):
     x, z, c = lax.axis_index("x"), lax.axis_index("z"), lax.axis_index("c")
     zh, y = lax.axis_index("zh"), lax.axis_index("y")
@@ -81,13 +82,36 @@
         )
 
     barrier = pltpu.get_barrier_semaphore()
-    everyone = [{"c": 1 - c}] + [{"x": p} for p in x_peers] + [{"z": p} for p in z_peers] + head_peers
-    for peer in everyone:
-        pl.semaphore_signal(barrier, inc=1, device_id=peer, device_id_type=pl.DeviceIdType.MESH)
+    across = [
+        {"zh": lax.div(p, 4), "z": lax.rem(p, 4)}
+        for p in (lax.rem(zh * 4 + z + 1, 8), lax.rem(zh * 4 + z + 7, 8))
+    ]
+    y_peers = [{"y": lax.rem(y + o, 4)} for o in (1, 2, 3)]
+    near = [{"c": 1 - c}] + [{"x": p} for p in x_peers] + [{"z": p} for p in z_peers] + y_peers + across
+
+    def signal_all(sem, peers):
+        for peer in peers:
+            pl.semaphore_signal(sem, inc=1, device_id=peer, device_id_type=pl.DeviceIdType.MESH)
+
+    signal_all(barrier, near)
+    inputs = [
+        pltpu.make_async_copy(src, dst, in_sems.at[i])
+        for i, (src, dst) in enumerate(
+            (
+                (gpos_hbm, gpos_ref), (k_hbm, k_ref), (v_hbm, v_ref), (keep_hbm, keep_ref),
+                (gain_hbm, gain_ref), (q_hbm, q_ref), (ct_hbm, ct_ref),
+            )
+        )
+    ]
+    for copy in inputs:
+        copy.start()
+    for copy in inputs[:4]:
+        copy.wait()
 
     offset = (x * 8 + z * 2 + c) * R
     rows = lax.broadcasted_iota(jnp.int32, (R, G), 0)
-    chosen = (jnp.broadcast_to(gpos_ref[...], (R, G)) - offset == rows).astype(F32).astype(BF)
+    wanted = jnp.concatenate([jnp.broadcast_to(gpos_ref[j : j + 1], (R, HD)) for j in range(G // HD)], 1)
+    chosen = (wanted - offset == rows).astype(F32).astype(BF)
     own_kv = jnp.concatenate([k_ref[...], v_ref[...]], 1)
     ga[0] = tn(chosen, own_kv).astype(BF).reshape(2, G // 2, 2 * HD)
     keep_rows = jnp.broadcast_to(keep_ref[...], (8, R)).astype(F32).astype(BF)
@@ -98,7 +122,8 @@
     ks[0:R] = k_ref[...]
     vs[0:R] = v_ref[...]
 
-    pl.semaphore_wait(barrier, len(everyone))
+    pl.semaphore_wait(barrier, len(near))
+    signal_all(ring_sem, across)
 
     def kv_copies(b):
         lower = R * (b + 1)
@@ -168,7 +193,7 @@
             for i, p in enumerate(peers)
         ]
 
-    def forward_group(g, bias):
+    def forward_group(g, bias, after=None):
         blocks = [BLOCKS[b] for b in GROUPS[g]]
 
         def body(h, carry):
@@ -195,15 +220,19 @@
             m_s[g, h] = peak
             l_s[g, h] = jnp.broadcast_to(jnp.sum(total, 1, keepdims=True), (R, 128))
             o_s[g, h] = mixed
+            if after is not None:
+                after(h)
             return carry
 
         lax.fori_loop(0, H, body, 0, unroll=2)
 
-    def backward_group(g, first):
+    def backward_group(g, before=None):
         blocks = [BLOCKS[b] for b in GROUPS[g]]
 
         def body(h, carry):
             q = q_ref[:, head_cols(h)]
+            if before is not None:
+                before(h)
             factor = f_s[g, h]
             grad = (d_attn[h] * factor).astype(BF)
             shift = diag[h] * factor
@@ -217,7 +246,7 @@
                 d_query = term if d_query is None else d_query + term
                 dks[:, lower : lower + size] += nn(q_t, d_scores)
                 dvs[:, lower : lower + size] += nn(grad_t, e)
-            if first:
+            if before is not None:
                 dqs[h] = d_query
             else:
                 dqs[h] += d_query
@@ -232,22 +261,27 @@
 
     core0 = started([core_stage(0)] + flag_stage(0))
     kv = {b: started(kv_copies(b)) for b in (0, 1)}
+    for copy in inputs[4:]:
+        copy.wait()
+    gains[...] = gain_ref[...].astype(F32)
     waited(core0)
     add_core(0)
     fl[1] = fl[0] + flc[...]
     x0 = started(x_stage(0) + flag_stage(1))
     kv[3] = started(kv_copies(3))
-    kv[4] = started(kv_copies(4))
     forward_group(0, {})
+    pl.semaphore_wait(ring_sem, 2)
     waited(x0)
     add_x(0)
     fl[2] = fl[1] + flx[0] + flx[1] + flx[2]
     z0 = started(z_stage(0) + flag_stage(2))
+    kv[4] = started(kv_copies(4))
     kv[2] = started(kv_copies(2))
     waited(kv[0])
     waited(kv[1])
     forward_group(1, block_bias(1, 2))
     waited(z0)
+    signal_all(y_sem, y_peers)
     add_z(0)
     global_keep = fl[2] + flz[0] + flz[1] + flz[2]
     xb0 = started(x_back(0))
@@ -265,10 +299,11 @@
         ks[lower : lower + G // 2] = full[0, half, :, :HD]
         vs[lower : lower + G // 2] = full[0, half, :, HD:]
     global_bias = jnp.where(global_keep[0:1] > 0.5, 0.0, NEG_FILL)
-    forward_group(4, {6 * R: global_bias})
-
-    def merge(h, carry):
-        squares, crossed = carry
+    pl.semaphore_wait(y_sem, 3)
+    squares[...] = jnp.zeros_like(squares)
+    crossed[...] = jnp.zeros_like(crossed)
+
+    def merge(h):
         peaks = [m_s[g, h] for g in range(len(GROUPS))]
         peak = functools.reduce(jnp.maximum, peaks)
         weights = [jnp.exp2(p - peak) for p in peaks]
@@ -281,14 +316,14 @@
             term = factor * o_s[g, h]
             out = term if out is None else out + term
         attn[h] = out
-        up = ct_ref[:, head_cols(h)].astype(F32) * gain_ref[:, head_cols(h)].astype(F32)
-        return (squares + out * out, crossed + up * out)
-
-    zeros = jnp.zeros((R, HD), F32)
-    squares, crossed = lax.fori_loop(0, H, merge, (zeros, zeros))
+        up = ct_ref[:, head_cols(h)].astype(F32) * gains[pl.ds(h, 1)]
+        squares[...] += out * out
+        crossed[...] += up * out
+
+    forward_group(4, {6 * R: global_bias}, merge)
     rows8 = lax.broadcasted_iota(jnp.int32, (8, R), 0)
-    squares_row = jnp.broadcast_to(jnp.sum(squares.T, 0, keepdims=True), (8, R))
-    crossed_row = jnp.broadcast_to(jnp.sum(crossed.T, 0, keepdims=True), (8, R))
+    squares_row = jnp.broadcast_to(jnp.sum(squares[...].T, 0, keepdims=True), (8, R))
+    crossed_row = jnp.broadcast_to(jnp.sum(crossed[...].T, 0, keepdims=True), (8, R))
     st[...] = jnp.where(rows8 == 0, squares_row, crossed_row)
     stats = started(
         [
@@ -302,22 +337,17 @@
     both = st[...]
     for i in range(7):
         both = both + st_in[i]
-    inverse = lax.rsqrt(both[0:1] / FEATURES + NORM_EPS)
-    coef = inverse * inverse * inverse * both[1:2] / FEATURES
-    inverse = jnp.broadcast_to(inverse, (HD, R)).T
-    coef = jnp.broadcast_to(coef, (HD, R)).T
-
-    def norm_grad(h, carry):
+    inverse_row = lax.rsqrt(both[0:1] / FEATURES + NORM_EPS)
+    coef_row = inverse_row * inverse_row * inverse_row * both[1:2] / FEATURES
+    inverse[...] = jnp.broadcast_to(inverse_row, (HD, R)).T
+    coef[...] = jnp.broadcast_to(coef_row, (HD, R)).T
+
+    def norm_grad(h):
         out = attn[h]
-        gain = gain_ref[:, head_cols(h)].astype(F32)
-        up = ct_ref[:, head_cols(h)].astype(F32) * gain
-        grad = inverse * up - out * coef
+        up = ct_ref[:, head_cols(h)].astype(F32) * gains[pl.ds(h, 1)]
+        grad = inverse[...] * up - out * coef[...]
         d_attn[h] = grad
         diag[h] = jnp.broadcast_to(jnp.sum(grad * out, 1, keepdims=True), (R, HD))
-        normed_ref[:, head_cols(h)] = (out * inverse * gain).astype(BF)
-        return carry
-
-    lax.fori_loop(0, H, norm_grad, 0)
 
     def send_grads(b):
         lower = R * (b + 1)
@@ -327,29 +357,30 @@
             [remote(grad_out.at[b], grad_in.at[b], gr_send.at[b], gr_recv.at[b], partners[b])]
         )
 
-    backward_group(4, True)
+    backward_group(4, norm_grad)
     d_global = jnp.concatenate([dks[:, 6 * R :] * SCALE, dvs[:, 6 * R :]], 0).T
     ga[1] = d_global.astype(BF).reshape(2, G // 2, 2 * HD)
     core1 = started([core_stage(1)])
-    backward_group(3, False)
+    backward_group(3)
     waited(core1)
     add_core(1)
     x1 = started(x_stage(1))
     sent = send_grads(4)
-    backward_group(2, False)
+    backward_group(2)
     waited(x1)
     add_x(1)
     z1 = started(z_stage(1))
     sent += send_grads(2) + send_grads(3)
-    backward_group(1, False)
+    backward_group(1)
     waited(z1)
     add_z(1)
     xb1 = started(x_back(1))
     sent += send_grads(1) + send_grads(0)
-    backward_group(0, False)
+    backward_group(0)
 
     def finish(h, carry):
         dq_ref[:, head_cols(h)] = (dqs[h] * SCALE).astype(BF)
+        normed_ref[:, head_cols(h)] = (attn[h] * inverse[...] * gains[pl.ds(h, 1)]).astype(BF)
         return carry
 
     lax.fori_loop(0, H, finish, 0)
@@ -368,11 +399,28 @@
     dv_ref[...] = (d_values.T + back[:, HD:]).astype(BF)
 
 
+def hand_over(*refs):
+    sems = refs[8]
+    copies = [pltpu.make_async_copy(refs[i], refs[4 + i], sems.at[i]) for i in range(4)]
+    for copy in copies:
+        copy.start()
+    for copy in copies:
+        copy.wait()
+
+
 def per_device(queries, keys, values, key_keep, global_positions, gain, cotangent):
     vmem = pl.BlockSpec(memory_space=pltpu.VMEM)
     ng = len(GROUPS)
     half, eighth, width = G // 2, G // 8, 2 * HD
     scratch = [
+        pltpu.VMEM(queries.shape, BF),
+        pltpu.VMEM(keys.shape, BF),
+        pltpu.VMEM(values.shape, BF),
+        pltpu.VMEM((1, R), jnp.int32),
+        pltpu.VMEM((G // HD, HD), jnp.int32),
+        pltpu.VMEM((H, HD), BF),
+        pltpu.VMEM(cotangent.shape, BF),
+        pltpu.SemaphoreType.DMA((7,)),
         pltpu.VMEM((SLOTS, HD), BF),
         pltpu.VMEM((SLOTS, HD), BF),
         pltpu.VMEM((5, 1, R), jnp.int32),
@@ -393,17 +441,21 @@
         pltpu.VMEM((8, G), F32),
         pltpu.VMEM((3, 8, G), F32),
         pltpu.VMEM((3, 8, G), F32),
+        pltpu.VMEM((H, HD), F32),
+        *[pltpu.VMEM((R, HD), F32)] * 4,
         pltpu.VMEM((8, R), F32),
         pltpu.VMEM((7, 8, R), F32),
         pltpu.VMEM((5, 2, HD, R), BF),
         pltpu.VMEM((5, 2, HD, R), BF),
+        pltpu.SemaphoreType.REGULAR,
+        pltpu.SemaphoreType.REGULAR,
         *[pltpu.SemaphoreType.DMA((3, 5))] * 2,
         *[pltpu.SemaphoreType.DMA((2, 11))] * 2,
         *[pltpu.SemaphoreType.DMA((7,))] * 2,
         *[pltpu.SemaphoreType.DMA((7,))] * 2,
         *[pltpu.SemaphoreType.DMA((5,))] * 2,
     ]
-    return pl.pallas_call(
+    results = pl.pallas_call(
         kernel,
         out_shape=(
             jax.ShapeDtypeStruct(queries.shape, BF),
@@ -411,22 +463,37 @@
             jax.ShapeDtypeStruct(keys.shape, BF),
             jax.ShapeDtypeStruct(values.shape, BF),
         ),
-        in_specs=[vmem] * 7,
+        in_specs=[pl.BlockSpec(memory_space=pltpu.HBM)] * 7,
         out_specs=[vmem] * 4,
         scratch_shapes=scratch,
         compiler_params=pltpu.CompilerParams(
-            collective_id=0, has_side_effects=True, vmem_limit_bytes=60 << 20
+            collective_id=0, has_side_effects=True, vmem_limit_bytes=42 << 20
         ),
         name="butterfly",
     )(
-        queries,
-        keys,
-        values,
-        key_keep.reshape(1, R),
-        global_positions.reshape(1, G),
-        gain.reshape(1, -1),
-        cotangent,
+        *[
+            pltpu.with_memory_space_constraint(a, pltpu.HBM)
+            for a in (
+                queries,
+                keys,
+                values,
+                key_keep.reshape(1, R),
+                global_positions.reshape(G // HD, HD),
+                gain.reshape(H, HD),
+                cotangent,
+            )
+        ]
     )
+    anywhere = pl.BlockSpec(memory_space=pl.ANY)
+    return pl.pallas_call(
+        hand_over,
+        out_shape=tuple(jax.ShapeDtypeStruct(r.shape, r.dtype) for r in results),
+        in_specs=[anywhere] * 4,
+        out_specs=[anywhere] * 4,
+        scratch_shapes=[pltpu.SemaphoreType.DMA((4,))],
+        compiler_params=pltpu.CompilerParams(vmem_limit_bytes=1 << 20),
+        name="hand_over",
+    )(*results)
 
 
 def solution(mesh):

time: 73.4 us -> 64.9 us (0.88)
  local copies, waits for them, and re-layouts: 6.13 us -> 0 us
  Pallas kernels: 66.3 us -> 64.2 us
    unnamed x12 -> x0, local copies, waits for them, and re-layouts: 4.29 us -> none
    pallas_call x1, Pallas kernels: 66.3 us -> 63.1 us  [per_device(): pl.pallas_call(kernel, out_shape=(jax.ShapeDtypeStruct(queries.shape, BF)...]
    reshape x2 -> x0, local copies, waits for them, and re-layouts: 1.85 us -> none  [the longest x1 1.25 us: per_device(): global_positions.reshape(1, G)]
    pallas_call x0 -> x1, Pallas kernels: none -> 1.03 us  [per_device(): pl.pallas_call(hand_over, out_shape=tuple((jax.ShapeDtypeStruct(r.shape,...]
where the time goes in v2:
time: 64.9 us; the launch traced here: 64.8 us
  Pallas kernels  64.2 us (99%)
    pallas_call x1, Pallas kernels, per_device(): pl.pallas_call(kernel, out_shape=(jax.ShapeDtypeStruct(queries.shape, BF)...  63.1 us

profile of v2, /device:TPU:1, one launch (start us, length us, event | category | flops | bytes accessed | tf_op | source)
XLA Modules:
  0.0 64.8 jit_solution(6496203585741510309)
XLA Ops:
  0.6 63.1 %butterfly.1 = (bf16[256,1024]{1,0:T(8,128)(2,1)S(1)}, bf16[256,1024]{1,0:T(8,128)(2,1)S(1)}, bf16[256,128]{1,0:T(8,128)(2,1)S(1)}, bf16[256,128]{1,0:T(8,128)(2,1)S(1)}) custom-call(bf16[256,1024]{1,0:T(8,128)(2,1)} %q_hbm.1, bf16[256,128]{1,0:T(8,128)(2,1)} %k_hbm.1, bf16[256,128]{1,0:T(8,128)(2,1)} %v_hbm.1, s32[1,256]{1,0:T(1,128)} %bitcast.5, ...), custom_call_target="tpu_custom_call" | custom-call | tf_op jit(solution)/shard_map/butterfly/pallas_call | solution.py:458
  63.8 1.0 %hand_over.1 = (bf16[256,1024]{1,0:T(8,128)(2,1)}, bf16[256,1024]{1,0:T(8,128)(2,1)}, bf16[256,128]{1,0:T(8,128)(2,1)}, bf16[256,128]{1,0:T(8,128)(2,1)}) custom-call(bf16[256,1024]{1,0:T(8,128)(2,1)S(1)} %get-tuple-element.8.refs_0_, bf16[256,1024]{1,0:T(8,128)(2,1)S(1)} %get-tuple-element.9.refs_1_, bf16[256,128]{1,0:T(8,128)(2,1)S(1)} %get-tuple-element.10.refs_2_, ...), custom_call_target="tpu_custom_call" | custom-call | tf_op jit(solution)/shard_map/hand_over/pallas_call | solution.py:488

commit v3 on v2

--- a/solution.py
+++ b/solution.py
@@ -24,7 +24,7 @@
 SLOTS = 6 * R + G
 
 BLOCKS = [(R * i, R) for i in range(6)] + [(6 * R, G)]
-GROUPS = [(0,), (1, 2), (4, 3), (5,), (6,)]
+GROUPS = [(0, 1), (2, 4), (5, 3), (6,)]
 
 
 def nt(a, b):
@@ -52,14 +52,20 @@
     normed_ref, dq_ref, dk_ref, dv_ref,
     q_ref, k_ref, v_ref, keep_ref, gpos_ref, gain_ref, ct_ref, in_sems,
     ks, vs, keeps, own_bias, expo, m_s, l_s, o_s, f_s, attn, d_attn, diag, dqs, dks, dvs,
-    ga, gc, hb, gx, pb, gz, hfull, full,
-    fl, flc, flx, flz,
+    ga, gx, pb, gz, full, q_t,
+    fl, flx, flz,
     gains, squares, crossed, inverse, coef, st, st_in, grad_out, grad_in,
     ring_sem, y_sem, kv_send, kv_recv, g_send, g_recv, f_send, f_recv, st_send, st_recv, gr_send, gr_recv,
 ):
     x, z, c = lax.axis_index("x"), lax.axis_index("z"), lax.axis_index("c")
     zh, y = lax.axis_index("zh"), lax.axis_index("y")
-    x_peers = [lax.rem(x + o, 4) for o in (1, 2, 3)]
+    plane_peers = [
+        {"x": lax.rem(x + dx, 4), "c": c if dc == 0 else 1 - c}
+        for dx in (2, 1, 3, 0)
+        for dc in range(2)
+        if dx or dc
+    ]
+    me = 2 * x + c
     z_peers = [lax.rem(z + o, 4) for o in (1, 2, 3)]
     head_peers = [
         {"zh": lax.rem(zh + dz, 2), "y": lax.rem(y + dy, 4)}
@@ -87,7 +93,7 @@
         for p in (lax.rem(zh * 4 + z + 1, 8), lax.rem(zh * 4 + z + 7, 8))
     ]
     y_peers = [{"y": lax.rem(y + o, 4)} for o in (1, 2, 3)]
-    near = [{"c": 1 - c}] + [{"x": p} for p in x_peers] + [{"z": p} for p in z_peers] + y_peers + across
+    near = plane_peers + [{"z": p} for p in z_peers] + y_peers + across
 
     def signal_all(sem, peers):
         for peer in peers:
@@ -113,9 +119,9 @@
     wanted = jnp.concatenate([jnp.broadcast_to(gpos_ref[j : j + 1], (R, HD)) for j in range(G // HD)], 1)
     chosen = (wanted - offset == rows).astype(F32).astype(BF)
     own_kv = jnp.concatenate([k_ref[...], v_ref[...]], 1)
-    ga[0] = tn(chosen, own_kv).astype(BF).reshape(2, G // 2, 2 * HD)
+    ga[0] = tn(chosen, own_kv).astype(BF).reshape(8, G // 8, 2 * HD)
     keep_rows = jnp.broadcast_to(keep_ref[...], (8, R)).astype(F32).astype(BF)
-    fl[0] = nn(keep_rows, chosen)
+    fl[0] = nn(keep_rows, chosen)[0:1]
     eye = lax.broadcasted_iota(jnp.int32, (R, R), 0) == lax.broadcasted_iota(jnp.int32, (R, R), 1)
     row_bias = jnp.where(jnp.broadcast_to(keep_ref[...], (R, R)) == 1, 0.0, NEG_FILL)
     own_bias[...] = jnp.where(eye, 0.0, row_bias)
@@ -142,37 +148,27 @@
         for copy in copies:
             copy.wait()
 
-    def core_stage(t):
-        return remote(ga.at[t, 1 - c], gc.at[t], g_send.at[t, 0], g_recv.at[t, 0], {"c": 1 - c})
-
-    def x_stage(t):
+    def plane_stage(t):
         return [
-            remote(hb.at[t, p], gx.at[t, i], g_send.at[t, 1 + i], g_recv.at[t, 1 + i], {"x": p})
-            for i, p in enumerate(x_peers)
+            remote(ga.at[t, 2 * p["x"] + p["c"]], gx.at[t, i], g_send.at[t, i], g_recv.at[t, i], p)
+            for i, p in enumerate(plane_peers)
         ]
 
     def z_stage(t):
         return [
-            remote(pb.at[t], gz.at[t, i], g_send.at[t, 4 + i], g_recv.at[t, 4 + i], {"z": p})
+            remote(pb.at[t], gz.at[t, i], g_send.at[t, 7 + i], g_recv.at[t, 7 + i], {"z": p})
             for i, p in enumerate(z_peers)
         ]
 
-    def x_back(t):
+    def plane_back(t):
         return [
-            remote(hfull.at[t, x], hfull.at[t, x], g_send.at[t, 7 + i], g_recv.at[t, 7 + i], {"x": p})
-            for i, p in enumerate(x_peers)
-        ]
-
-    def core_back(t):
-        return remote(full.at[t, c], full.at[t, c], g_send.at[t, 10], g_recv.at[t, 10], {"c": 1 - c})
-
-    def add_core(t):
-        total = ga[t, c].astype(F32) + gc[t].astype(F32)
-        hb[t] = total.astype(BF).reshape(4, G // 8, 2 * HD)
-
-    def add_x(t):
-        total = hb[t, x].astype(F32)
-        for i in range(3):
+            remote(full.at[t, me], full.at[t, me], g_send.at[t, 10 + i], g_recv.at[t, 10 + i], p)
+            for i, p in enumerate(plane_peers)
+        ]
+
+    def add_plane(t):
+        total = ga[t, me].astype(F32)
+        for i in range(7):
             total = total + gx[t, i].astype(F32)
         pb[t] = total.astype(BF)
 
@@ -180,14 +176,11 @@
         total = pb[t].astype(F32)
         for i in range(3):
             total = total + gz[t, i].astype(F32)
-        hfull[t, x] = total.astype(BF)
+        full[t, me] = total.astype(BF)
 
     def flag_stage(s):
-        if s == 0:
-            return [remote(fl.at[0], flc, f_send.at[0], f_recv.at[0], {"c": 1 - c})]
-        peers = [{"x": p} for p in x_peers] if s == 1 else [{"z": p} for p in z_peers]
-        into = flx if s == 1 else flz
-        base = 1 if s == 1 else 4
+        peers = plane_peers if s == 0 else [{"z": p} for p in z_peers]
+        into, base = (flx, 0) if s == 0 else (flz, 7)
         return [
             remote(fl.at[s], into.at[i], f_send.at[base + i], f_recv.at[base + i], p)
             for i, p in enumerate(peers)
@@ -226,17 +219,16 @@
 
         lax.fori_loop(0, H, body, 0, unroll=2)
 
-    def backward_group(g, before=None):
-        blocks = [BLOCKS[b] for b in GROUPS[g]]
+    def backward_group(g, numbers, before=None):
+        blocks = [BLOCKS[b] for b in numbers]
 
         def body(h, carry):
-            q = q_ref[:, head_cols(h)]
             if before is not None:
                 before(h)
             factor = f_s[g, h]
             grad = (d_attn[h] * factor).astype(BF)
             shift = diag[h] * factor
-            q_t, grad_t = q.T, grad.T
+            grad_t = grad.T
             d_query = None
             for lower, size in blocks:
                 e = expo[h, :, lower : lower + size]
@@ -244,7 +236,7 @@
                 d_scores = (e.astype(F32) * (d_probs - wide(shift, size))).astype(BF)
                 term = nn(d_scores, ks[lower : lower + size])
                 d_query = term if d_query is None else d_query + term
-                dks[:, lower : lower + size] += nn(q_t, d_scores)
+                dks[:, lower : lower + size] += nn(q_t[h], d_scores)
                 dvs[:, lower : lower + size] += nn(grad_t, e)
             if before is not None:
                 dqs[h] = d_query
@@ -259,45 +251,38 @@
             BLOCKS[b][0]: jnp.where(keeps[b - 1] == 1, 0.0, NEG_FILL).astype(F32) for b in numbers
         }
 
-    core0 = started([core_stage(0)] + flag_stage(0))
-    kv = {b: started(kv_copies(b)) for b in (0, 1)}
+    plane0 = started(plane_stage(0) + flag_stage(0))
+    kv = {b: started(kv_copies(b)) for b in (0, 1, 3, 4)}
     for copy in inputs[4:]:
         copy.wait()
     gains[...] = gain_ref[...].astype(F32)
-    waited(core0)
-    add_core(0)
-    fl[1] = fl[0] + flc[...]
-    x0 = started(x_stage(0) + flag_stage(1))
-    kv[3] = started(kv_copies(3))
-    forward_group(0, {})
+    waited(kv[0])
+    forward_group(0, block_bias(1))
     pl.semaphore_wait(ring_sem, 2)
-    waited(x0)
-    add_x(0)
-    fl[2] = fl[1] + flx[0] + flx[1] + flx[2]
-    z0 = started(z_stage(0) + flag_stage(2))
-    kv[4] = started(kv_copies(4))
+    waited(plane0)
+    add_plane(0)
+    keep_plane = fl[0]
+    for i in range(7):
+        keep_plane = keep_plane + flx[i]
+    fl[1] = keep_plane
+    z0 = started(z_stage(0) + flag_stage(1))
     kv[2] = started(kv_copies(2))
-    waited(kv[0])
     waited(kv[1])
-    forward_group(1, block_bias(1, 2))
+    waited(kv[3])
+    forward_group(1, block_bias(2, 4))
     waited(z0)
     signal_all(y_sem, y_peers)
     add_z(0)
-    global_keep = fl[2] + flz[0] + flz[1] + flz[2]
-    xb0 = started(x_back(0))
-    waited(kv[3])
+    global_keep = fl[1] + flz[0] + flz[1] + flz[2]
+    back0 = started(plane_back(0))
+    waited(kv[4])
     waited(kv[2])
-    forward_group(2, block_bias(4, 3))
-    waited(xb0)
-    full[0, c] = hfull[0].reshape(G // 2, 2 * HD)
-    cb0 = started([core_back(0)])
-    waited(kv[4])
-    forward_group(3, block_bias(5))
-    waited(cb0)
-    for half in range(2):
-        lower = 6 * R + half * (G // 2)
-        ks[lower : lower + G // 2] = full[0, half, :, :HD]
-        vs[lower : lower + G // 2] = full[0, half, :, HD:]
+    forward_group(2, block_bias(5, 3))
+    waited(back0)
+    lower = 6 * R
+    all_kv = full[0].reshape(G, 2 * HD)
+    ks[lower : lower + G] = all_kv[:, :HD]
+    vs[lower : lower + G] = all_kv[:, HD:]
     global_bias = jnp.where(global_keep[0:1] > 0.5, 0.0, NEG_FILL)
     pl.semaphore_wait(y_sem, 3)
     squares[...] = jnp.zeros_like(squares)
@@ -320,7 +305,7 @@
         squares[...] += out * out
         crossed[...] += up * out
 
-    forward_group(4, {6 * R: global_bias}, merge)
+    forward_group(3, {6 * R: global_bias}, merge)
     rows8 = lax.broadcasted_iota(jnp.int32, (8, R), 0)
     squares_row = jnp.broadcast_to(jnp.sum(squares[...].T, 0, keepdims=True), (8, R))
     crossed_row = jnp.broadcast_to(jnp.sum(crossed[...].T, 0, keepdims=True), (8, R))
@@ -331,6 +316,12 @@
             for i, peer in enumerate(head_peers)
         ]
     )
+
+    def transpose_queries(h, carry):
+        q_t[h] = q_ref[:, head_cols(h)].T
+        return carry
+
+    lax.fori_loop(0, H, transpose_queries, 0, unroll=2)
     dks[...] = jnp.zeros_like(dks)
     dvs[...] = jnp.zeros_like(dvs)
     waited(stats)
@@ -357,26 +348,23 @@
             [remote(grad_out.at[b], grad_in.at[b], gr_send.at[b], gr_recv.at[b], partners[b])]
         )
 
-    backward_group(4, norm_grad)
+    backward_group(3, (6,), norm_grad)
     d_global = jnp.concatenate([dks[:, 6 * R :] * SCALE, dvs[:, 6 * R :]], 0).T
-    ga[1] = d_global.astype(BF).reshape(2, G // 2, 2 * HD)
-    core1 = started([core_stage(1)])
-    backward_group(3)
-    waited(core1)
-    add_core(1)
-    x1 = started(x_stage(1))
+    ga[1] = d_global.astype(BF).reshape(8, G // 8, 2 * HD)
+    plane1 = started(plane_stage(1))
+    backward_group(2, (5, 3))
     sent = send_grads(4)
-    backward_group(2)
-    waited(x1)
-    add_x(1)
+    waited(plane1)
+    add_plane(1)
     z1 = started(z_stage(1))
-    sent += send_grads(2) + send_grads(3)
-    backward_group(1)
+    sent += send_grads(2)
+    backward_group(1, (4, 2))
+    sent += send_grads(3) + send_grads(1)
     waited(z1)
     add_z(1)
-    xb1 = started(x_back(1))
-    sent += send_grads(1) + send_grads(0)
-    backward_group(0)
+    back1 = started(plane_back(1))
+    backward_group(0, (1, 0))
+    sent += send_grads(0)
 
     def finish(h, carry):
         dq_ref[:, head_cols(h)] = (dqs[h] * SCALE).astype(BF)
@@ -384,16 +372,13 @@
         return carry
 
     lax.fori_loop(0, H, finish, 0)
-    waited(xb1)
-    full[1, c] = hfull[1].reshape(G // 2, 2 * HD)
-    cb1 = started([core_back(1)])
     waited(sent)
     d_keys = dks[:, 0:R] * SCALE
     d_values = dvs[:, 0:R]
     for b in range(5):
         d_keys = d_keys + grad_in[b, 0].astype(F32)
         d_values = d_values + grad_in[b, 1].astype(F32)
-    waited(cb1)
+    waited(back1)
     back = nn(chosen, full[1].reshape(G, 2 * HD))
     dk_ref[...] = (d_keys.T + back[:, :HD]).astype(BF)
     dv_ref[...] = (d_values.T + back[:, HD:]).astype(BF)
@@ -411,7 +396,7 @@
 def per_device(queries, keys, values, key_keep, global_positions, gain, cotangent):
     vmem = pl.BlockSpec(memory_space=pltpu.VMEM)
     ng = len(GROUPS)
-    half, eighth, width = G // 2, G // 8, 2 * HD
+    eighth, width = G // 8, 2 * HD
     scratch = [
         pltpu.VMEM(queries.shape, BF),
         pltpu.VMEM(keys.shape, BF),
@@ -429,18 +414,15 @@
         *[pltpu.VMEM((ng, H, R, HD), F32)] * 4,
         *[pltpu.VMEM((H, R, HD), F32)] * 4,
         *[pltpu.VMEM((HD, SLOTS), F32)] * 2,
-        pltpu.VMEM((2, 2, half, width), BF),
-        pltpu.VMEM((2, half, width), BF),
-        pltpu.VMEM((2, 4, eighth, width), BF),
-        pltpu.VMEM((2, 3, eighth, width), BF),
+        pltpu.VMEM((2, 8, eighth, width), BF),
+        pltpu.VMEM((2, 7, eighth, width), BF),
         pltpu.VMEM((2, eighth, width), BF),
         pltpu.VMEM((2, 3, eighth, width), BF),
-        pltpu.VMEM((2, 4, eighth, width), BF),
-        pltpu.VMEM((2, 2, half, width), BF),
-        pltpu.VMEM((3, 8, G), F32),
-        pltpu.VMEM((8, G), F32),
-        pltpu.VMEM((3, 8, G), F32),
-        pltpu.VMEM((3, 8, G), F32),
+        pltpu.VMEM((2, 8, eighth, width), BF),
+        pltpu.VMEM((H, HD, R), BF),
+        pltpu.VMEM((2, 1, G), F32),
+        pltpu.VMEM((7, 1, G), F32),
+        pltpu.VMEM((3, 1, G), F32),
         pltpu.VMEM((H, HD), F32),
         *[pltpu.VMEM((R, HD), F32)] * 4,
         pltpu.VMEM((8, R), F32),
@@ -450,8 +432,8 @@
         pltpu.SemaphoreType.REGULAR,
         pltpu.SemaphoreType.REGULAR,
         *[pltpu.SemaphoreType.DMA((3, 5))] * 2,
-        *[pltpu.SemaphoreType.DMA((2, 11))] * 2,
-        *[pltpu.SemaphoreType.DMA((7,))] * 2,
+        *[pltpu.SemaphoreType.DMA((2, 17))] * 2,
+        *[pltpu.SemaphoreType.DMA((10,))] * 2,
         *[pltpu.SemaphoreType.DMA((7,))] * 2,
         *[pltpu.SemaphoreType.DMA((5,))] * 2,
     ]

time: 64.9 us -> 59.6 us (0.918)
  Pallas kernels: 64.2 us -> 58.9 us
    pallas_call x1, Pallas kernels: 63.1 us -> 57.8 us  [per_device(): pl.pallas_call(kernel, out_shape=(jax.ShapeDtypeStruct(queries.shape, BF)...]
where the time goes in v3:
time: 59.6 us; the launch traced here: 59.5 us
  Pallas kernels  58.9 us (99%)
  between operations  0.64 us (1%)
    pallas_call x1, Pallas kernels, per_device(): pl.pallas_call(kernel, out_shape=(jax.ShapeDtypeStruct(queries.shape, BF)...  57.8 us

profile of v3, /device:TPU:1, one launch (start us, length us, event | category | flops | bytes accessed | tf_op | source)
XLA Modules:
  0.0 59.5 jit_solution(6982679273987819509)
XLA Ops:
  0.6 57.8 %butterfly.1 = (bf16[256,1024]{1,0:T(8,128)(2,1)S(1)}, bf16[256,1024]{1,0:T(8,128)(2,1)S(1)}, bf16[256,128]{1,0:T(8,128)(2,1)S(1)}, bf16[256,128]{1,0:T(8,128)(2,1)S(1)}) custom-call(bf16[256,1024]{1,0:T(8,128)(2,1)} %q_hbm.1, bf16[256,128]{1,0:T(8,128)(2,1)} %k_hbm.1, bf16[256,128]{1,0:T(8,128)(2,1)} %v_hbm.1, s32[1,256]{1,0:T(1,128)} %bitcast.5, ...), custom_call_target="tpu_custom_call" | custom-call | tf_op jit(solution)/shard_map/butterfly/pallas_call | solution.py:440
  58.5 1.0 %hand_over.1 = (bf16[256,1024]{1,0:T(8,128)(2,1)}, bf16[256,1024]{1,0:T(8,128)(2,1)}, bf16[256,128]{1,0:T(8,128)(2,1)}, bf16[256,128]{1,0:T(8,128)(2,1)}) custom-call(bf16[256,1024]{1,0:T(8,128)(2,1)S(1)} %get-tuple-element.8.refs_0_, bf16[256,1024]{1,0:T(8,128)(2,1)S(1)} %get-tuple-element.9.refs_1_, bf16[256,128]{1,0:T(8,128)(2,1)S(1)} %get-tuple-element.10.refs_2_, ...), custom_call_target="tpu_custom_call" | custom-call | tf_op jit(solution)/shard_map/hand_over/pallas_call | solution.py:470

commit v4 on v3

--- a/solution.py
+++ b/solution.py
@@ -54,7 +54,7 @@
     ks, vs, keeps, own_bias, expo, m_s, l_s, o_s, f_s, attn, d_attn, diag, dqs, dks, dvs,
     ga, gx, pb, gz, full, q_t,
     fl, flx, flz,
-    gains, squares, crossed, inverse, coef, st, st_in, grad_out, grad_in,
+    up_sums, out_sums, xs, dq2, f_near, gains, squares, crossed, inverse, coef, st, st_in, grad_out, grad_in,
     ring_sem, y_sem, kv_send, kv_recv, g_send, g_recv, f_send, f_recv, st_send, st_recv, gr_send, gr_recv,
 ):
     x, z, c = lax.axis_index("x"), lax.axis_index("z"), lax.axis_index("c")
@@ -219,12 +219,10 @@
 
         lax.fori_loop(0, H, body, 0, unroll=2)
 
-    def backward_group(g, numbers, before=None):
+    def backward_group(g, numbers, first=False):
         blocks = [BLOCKS[b] for b in numbers]
 
         def body(h, carry):
-            if before is not None:
-                before(h)
             factor = f_s[g, h]
             grad = (d_attn[h] * factor).astype(BF)
             shift = diag[h] * factor
@@ -238,8 +236,8 @@
                 d_query = term if d_query is None else d_query + term
                 dks[:, lower : lower + size] += nn(q_t[h], d_scores)
                 dvs[:, lower : lower + size] += nn(grad_t, e)
-            if before is not None:
-                dqs[h] = d_query
+            if first:
+                dqs[h] = inverse[...] * dqs[h] - coef[...] * dq2[h] + d_query
             else:
                 dqs[h] += d_query
             return carry
@@ -252,7 +250,7 @@
         }
 
     plane0 = started(plane_stage(0) + flag_stage(0))
-    kv = {b: started(kv_copies(b)) for b in (0, 1, 3, 4)}
+    kv = {b: started(kv_copies(b)) for b in (0, 2, 3, 1, 4)}
     for copy in inputs[4:]:
         copy.wait()
     gains[...] = gain_ref[...].astype(F32)
@@ -266,7 +264,6 @@
         keep_plane = keep_plane + flx[i]
     fl[1] = keep_plane
     z0 = started(z_stage(0) + flag_stage(1))
-    kv[2] = started(kv_copies(2))
     waited(kv[1])
     waited(kv[3])
     forward_group(1, block_bias(2, 4))
@@ -278,6 +275,20 @@
     waited(kv[4])
     waited(kv[2])
     forward_group(2, block_bias(5, 3))
+
+    def merge_near(h, carry):
+        peaks = [m_s[g, h] for g in range(3)]
+        peak = functools.reduce(jnp.maximum, peaks)
+        total, out = None, None
+        for g, p in enumerate(peaks):
+            weight = jnp.exp2(p - peak)
+            f_s[g, h] = weight
+            total = weight * l_s[g, h] if g == 0 else total + weight * l_s[g, h]
+            out = weight * o_s[g, h] if g == 0 else out + weight * o_s[g, h]
+        m_s[0, h], l_s[0, h], o_s[0, h] = peak, total, out
+        return carry
+
+    lax.fori_loop(0, H, merge_near, 0)
     waited(back0)
     lower = 6 * R
     all_kv = full[0].reshape(G, 2 * HD)
@@ -289,17 +300,13 @@
     crossed[...] = jnp.zeros_like(crossed)
 
     def merge(h):
-        peaks = [m_s[g, h] for g in range(len(GROUPS))]
-        peak = functools.reduce(jnp.maximum, peaks)
-        weights = [jnp.exp2(p - peak) for p in peaks]
-        total = sum(w * l_s[g, h] for g, w in enumerate(weights))
-        inv_total = 1.0 / total
-        out = None
-        for g, w in enumerate(weights):
-            factor = w * inv_total
-            f_s[g, h] = factor
-            term = factor * o_s[g, h]
-            out = term if out is None else out + term
+        peak = jnp.maximum(m_s[0, h], m_s[3, h])
+        near_weight, far_weight = jnp.exp2(m_s[0, h] - peak), jnp.exp2(m_s[3, h] - peak)
+        inv_total = 1.0 / (near_weight * l_s[0, h] + far_weight * l_s[3, h])
+        near_weight, far_weight = near_weight * inv_total, far_weight * inv_total
+        f_near[h] = near_weight
+        f_s[3, h] = far_weight
+        out = near_weight * o_s[0, h] + far_weight * o_s[3, h]
         attn[h] = out
         up = ct_ref[:, head_cols(h)].astype(F32) * gains[pl.ds(h, 1)]
         squares[...] += out * out
@@ -317,11 +324,24 @@
         ]
     )
 
-    def transpose_queries(h, carry):
+    def prepare(h, carry):
         q_t[h] = q_ref[:, head_cols(h)].T
+        for g in range(3):
+            f_s[g, h] = f_s[g, h] * f_near[h]
+        factor, out = f_s[3, h], attn[h]
+        up = ct_ref[:, head_cols(h)].astype(F32) * gains[pl.ds(h, 1)]
+        up_sum = jnp.broadcast_to(jnp.sum(up * out, 1, keepdims=True), (R, HD))
+        out_sum = jnp.broadcast_to(jnp.sum(out * out, 1, keepdims=True), (R, HD))
+        up_sums[h], out_sums[h] = up_sum, out_sum
+        e = expo[h, :, 6 * R :].astype(F32)
+        x1 = (e * (nt((up * factor).astype(BF), vs[6 * R :]) - wide(up_sum * factor, G))).astype(BF)
+        x2 = (e * (nt((out * factor).astype(BF), vs[6 * R :]) - wide(out_sum * factor, G))).astype(BF)
+        xs[h, 0:R], xs[h, R : 2 * R] = x1, x2
+        dqs[h] = nn(x1, ks[6 * R :])
+        dq2[h] = nn(x2, ks[6 * R :])
         return carry
 
-    lax.fori_loop(0, H, transpose_queries, 0, unroll=2)
+    lax.fori_loop(0, H, prepare, 0, unroll=2)
     dks[...] = jnp.zeros_like(dks)
     dvs[...] = jnp.zeros_like(dvs)
     waited(stats)
@@ -333,12 +353,21 @@
     inverse[...] = jnp.broadcast_to(inverse_row, (HD, R)).T
     coef[...] = jnp.broadcast_to(coef_row, (HD, R)).T
 
-    def norm_grad(h):
+    inverse_t = jnp.broadcast_to(inverse_row, (HD, R))
+    coef_t = jnp.broadcast_to(-coef_row, (HD, R))
+
+    def global_grads(h, carry):
         out = attn[h]
         up = ct_ref[:, head_cols(h)].astype(F32) * gains[pl.ds(h, 1)]
         grad = inverse[...] * up - out * coef[...]
         d_attn[h] = grad
-        diag[h] = jnp.broadcast_to(jnp.sum(grad * out, 1, keepdims=True), (R, HD))
+        diag[h] = inverse[...] * up_sums[h] - coef[...] * out_sums[h]
+        queries = q_t[h].astype(F32)
+        both_t = jnp.concatenate([queries * inverse_t, queries * coef_t], 1).astype(BF)
+        dks[:, 6 * R :] += nn(both_t, xs[h])
+        grad_t = (grad * f_s[3, h]).astype(BF).T
+        dvs[:, 6 * R :] += nn(grad_t, expo[h, :, 6 * R :])
+        return carry
 
     def send_grads(b):
         lower = R * (b + 1)
@@ -348,11 +377,11 @@
             [remote(grad_out.at[b], grad_in.at[b], gr_send.at[b], gr_recv.at[b], partners[b])]
         )
 
-    backward_group(3, (6,), norm_grad)
-    d_global = jnp.concatenate([dks[:, 6 * R :] * SCALE, dvs[:, 6 * R :]], 0).T
-    ga[1] = d_global.astype(BF).reshape(8, G // 8, 2 * HD)
+    lax.fori_loop(0, H, global_grads, 0, unroll=2)
+    d_global = jnp.concatenate([dks[:, 6 * R :] * SCALE, dvs[:, 6 * R :]], 0).astype(BF).T
+    ga[1] = d_global.reshape(8, G // 8, 2 * HD)
     plane1 = started(plane_stage(1))
-    backward_group(2, (5, 3))
+    backward_group(2, (5, 3), True)
     sent = send_grads(4)
     waited(plane1)
     add_plane(1)
@@ -423,6 +452,9 @@
         pltpu.VMEM((2, 1, G), F32),
         pltpu.VMEM((7, 1, G), F32),
         pltpu.VMEM((3, 1, G), F32),
+        *[pltpu.VMEM((H, R, HD), F32)] * 2,
+        pltpu.VMEM((H, 2 * R, G), BF),
+        *[pltpu.VMEM((H, R, HD), F32)] * 2,
         pltpu.VMEM((H, HD), F32),
         *[pltpu.VMEM((R, HD), F32)] * 4,
         pltpu.VMEM((8, R), F32),
@@ -449,7 +481,7 @@
         out_specs=[vmem] * 4,
         scratch_shapes=scratch,
         compiler_params=pltpu.CompilerParams(
-            collective_id=0, has_side_effects=True, vmem_limit_bytes=42 << 20
+            collective_id=0, has_side_effects=True, vmem_limit_bytes=46 << 20
         ),
         name="butterfly",
     )(

time: 59.6 us -> 55.7 us (0.935)
  Pallas kernels: 58.9 us -> 54.9 us
    pallas_call x1, Pallas kernels: 57.8 us -> 53.9 us  [per_device(): pl.pallas_call(kernel, out_shape=(jax.ShapeDtypeStruct(queries.shape, BF)...]
where the time goes in v4:
time: 55.7 us; the launch traced here: 55.6 us
  Pallas kernels  54.9 us (99%)
  between operations  0.64 us (1%)
    pallas_call x1, Pallas kernels, per_device(): pl.pallas_call(kernel, out_shape=(jax.ShapeDtypeStruct(queries.shape, BF)...  53.9 us

profile of v4, /device:TPU:1, one launch (start us, length us, event | category | flops | bytes accessed | tf_op | source)
XLA Modules:
  0.0 55.6 jit_solution(12574977936427103204)
XLA Ops:
  0.6 53.9 %butterfly.1 = (bf16[256,1024]{1,0:T(8,128)(2,1)S(1)}, bf16[256,1024]{1,0:T(8,128)(2,1)S(1)}, bf16[256,128]{1,0:T(8,128)(2,1)S(1)}, bf16[256,128]{1,0:T(8,128)(2,1)S(1)}) custom-call(bf16[256,1024]{1,0:T(8,128)(2,1)} %q_hbm.1, bf16[256,128]{1,0:T(8,128)(2,1)} %k_hbm.1, bf16[256,128]{1,0:T(8,128)(2,1)} %v_hbm.1, s32[1,256]{1,0:T(1,128)} %bitcast.5, ...), custom_call_target="tpu_custom_call" | custom-call | tf_op jit(solution)/shard_map/butterfly/pallas_call | solution.py:472
  54.6 1.0 %hand_over.1 = (bf16[256,1024]{1,0:T(8,128)(2,1)}, bf16[256,1024]{1,0:T(8,128)(2,1)}, bf16[256,128]{1,0:T(8,128)(2,1)}, bf16[256,128]{1,0:T(8,128)(2,1)}) custom-call(bf16[256,1024]{1,0:T(8,128)(2,1)S(1)} %get-tuple-element.8.refs_0_, bf16[256,1024]{1,0:T(8,128)(2,1)S(1)} %get-tuple-element.9.refs_1_, bf16[256,128]{1,0:T(8,128)(2,1)S(1)} %get-tuple-element.10.refs_2_, ...), custom_call_target="tpu_custom_call" | custom-call | tf_op jit(solution)/shard_map/hand_over/pallas_call | solution.py:502

commit v5 on v4

--- a/solution.py
+++ b/solution.py
@@ -24,7 +24,7 @@
 SLOTS = 6 * R + G
 
 BLOCKS = [(R * i, R) for i in range(6)] + [(6 * R, G)]
-GROUPS = [(0, 1), (2, 4), (5, 3), (6,)]
+GROUPS = [(0, 1), (3, 2), (5, 4), (6,)]
 
 
 def nt(a, b):
@@ -186,38 +186,50 @@
             for i, p in enumerate(peers)
         ]
 
-    def forward_group(g, bias, after=None):
+    def forward_group(g, bias, after=None, heads=2):
         blocks = [BLOCKS[b] for b in GROUPS[g]]
 
-        def body(h, carry):
-            q = q_ref[:, head_cols(h)]
-            parts, top = [], None
-            for lower, size in blocks:
-                s = nt(q, ks[lower : lower + size])
-                s = s + (own_bias[...] if lower == 0 else bias[lower])
-                parts.append(s)
-                for j in range(0, size, 128):
-                    piece = s[:, j : j + 128]
-                    top = piece if top is None else jnp.maximum(top, piece)
-            peak = jnp.broadcast_to(jnp.max(top, 1, keepdims=True), (R, 128)) * SCALE2
-            mixed, total = None, None
-            for (lower, size), s in zip(blocks, parts):
-                e = jnp.exp2(s * SCALE2 - wide(peak, size))
-                for j in range(0, size, 128):
-                    piece = e[:, j : j + 128]
-                    total = piece if total is None else total + piece
-                e_bf = e.astype(BF)
-                expo[h, :, lower : lower + size] = e_bf
-                term = nn(e_bf, vs[lower : lower + size])
-                mixed = term if mixed is None else mixed + term
-            m_s[g, h] = peak
-            l_s[g, h] = jnp.broadcast_to(jnp.sum(total, 1, keepdims=True), (R, 128))
-            o_s[g, h] = mixed
+        def body(i, carry):
+            hs = [heads * i + j for j in range(heads)]
+            queries = [q_ref[:, head_cols(h)] for h in hs]
+            given = [after[0](h) for h in hs] if after is not None else None
+            scores = []
+            for q in queries:
+                parts = []
+                for lower, size in blocks:
+                    s = nt(q, ks[lower : lower + size])
+                    parts.append(s + (own_bias[...] if lower == 0 else bias[lower]))
+                scores.append(parts)
+            results = []
+            for parts in scores:
+                top = None
+                for s in parts:
+                    for j in range(0, s.shape[1], 128):
+                        piece = s[:, j : j + 128]
+                        top = piece if top is None else jnp.maximum(top, piece)
+                peak = jnp.broadcast_to(jnp.max(top, 1, keepdims=True), (R, 128)) * SCALE2
+                mixed, total, expos = None, None, []
+                for (lower, size), s in zip(blocks, parts):
+                    e = jnp.exp2(s * SCALE2 - wide(peak, size))
+                    for j in range(0, size, 128):
+                        piece = e[:, j : j + 128]
+                        total = piece if total is None else total + piece
+                    e_bf = e.astype(BF)
+                    expos.append(e_bf)
+                    term = nn(e_bf, vs[lower : lower + size])
+                    mixed = term if mixed is None else mixed + term
+                total = jnp.broadcast_to(jnp.sum(total, 1, keepdims=True), (R, 128))
+                results.append((peak, total, mixed, expos))
+            for h, (peak, total, mixed, expos) in zip(hs, results):
+                for (lower, size), e_bf in zip(blocks, expos):
+                    expo[h, :, lower : lower + size] = e_bf
+                if after is None:
+                    m_s[g, h], l_s[g, h], o_s[g, h] = peak, total, mixed
             if after is not None:
-                after(h)
+                after[1](hs, given, results)
             return carry
 
-        lax.fori_loop(0, H, body, 0, unroll=2)
+        lax.fori_loop(0, H // heads, body, 0)
 
     def backward_group(g, numbers, first=False):
         blocks = [BLOCKS[b] for b in numbers]
@@ -264,17 +276,17 @@
         keep_plane = keep_plane + flx[i]
     fl[1] = keep_plane
     z0 = started(z_stage(0) + flag_stage(1))
+    waited(kv[2])
     waited(kv[1])
-    waited(kv[3])
-    forward_group(1, block_bias(2, 4))
+    forward_group(1, block_bias(3, 2))
     waited(z0)
     signal_all(y_sem, y_peers)
     add_z(0)
     global_keep = fl[1] + flz[0] + flz[1] + flz[2]
     back0 = started(plane_back(0))
+    waited(kv[3])
     waited(kv[4])
-    waited(kv[2])
-    forward_group(2, block_bias(5, 3))
+    forward_group(2, block_bias(5, 4))
 
     def merge_near(h, carry):
         peaks = [m_s[g, h] for g in range(3)]
@@ -299,20 +311,27 @@
     squares[...] = jnp.zeros_like(squares)
     crossed[...] = jnp.zeros_like(crossed)
 
-    def merge(h):
-        peak = jnp.maximum(m_s[0, h], m_s[3, h])
-        near_weight, far_weight = jnp.exp2(m_s[0, h] - peak), jnp.exp2(m_s[3, h] - peak)
-        inv_total = 1.0 / (near_weight * l_s[0, h] + far_weight * l_s[3, h])
-        near_weight, far_weight = near_weight * inv_total, far_weight * inv_total
-        f_near[h] = near_weight
-        f_s[3, h] = far_weight
-        out = near_weight * o_s[0, h] + far_weight * o_s[3, h]
-        attn[h] = out
+    def merge_load(h):
         up = ct_ref[:, head_cols(h)].astype(F32) * gains[pl.ds(h, 1)]
-        squares[...] += out * out
-        crossed[...] += up * out
-
-    forward_group(3, {6 * R: global_bias}, merge)
+        return m_s[0, h], l_s[0, h], o_s[0, h], up
+
+    def merge(hs, given, results):
+        square, cross, kept = None, None, []
+        for (m0, l0, o0, up), (m3, l3, o3, _) in zip(given, results):
+            peak = jnp.maximum(m0, m3)
+            near_weight, far_weight = jnp.exp2(m0 - peak), jnp.exp2(m3 - peak)
+            inv_total = 1.0 / (near_weight * l0 + far_weight * l3)
+            near_weight, far_weight = near_weight * inv_total, far_weight * inv_total
+            out = near_weight * o0 + far_weight * o3
+            kept.append((near_weight, far_weight, out))
+            square = out * out if square is None else square + out * out
+            cross = up * out if cross is None else cross + up * out
+        for h, (near_weight, far_weight, out) in zip(hs, kept):
+            f_near[h], f_s[3, h], attn[h] = near_weight, far_weight, out
+        squares[...] += square
+        crossed[...] += cross
+
+    forward_group(3, {6 * R: global_bias}, (merge_load, merge), 4)
     rows8 = lax.broadcasted_iota(jnp.int32, (8, R), 0)
     squares_row = jnp.broadcast_to(jnp.sum(squares[...].T, 0, keepdims=True), (8, R))
     crossed_row = jnp.broadcast_to(jnp.sum(crossed[...].T, 0, keepdims=True), (8, R))
@@ -356,17 +375,25 @@
     inverse_t = jnp.broadcast_to(inverse_row, (HD, R))
     coef_t = jnp.broadcast_to(-coef_row, (HD, R))
 
-    def global_grads(h, carry):
-        out = attn[h]
-        up = ct_ref[:, head_cols(h)].astype(F32) * gains[pl.ds(h, 1)]
-        grad = inverse[...] * up - out * coef[...]
-        d_attn[h] = grad
-        diag[h] = inverse[...] * up_sums[h] - coef[...] * out_sums[h]
-        queries = q_t[h].astype(F32)
-        both_t = jnp.concatenate([queries * inverse_t, queries * coef_t], 1).astype(BF)
-        dks[:, 6 * R :] += nn(both_t, xs[h])
-        grad_t = (grad * f_s[3, h]).astype(BF).T
-        dvs[:, 6 * R :] += nn(grad_t, expo[h, :, 6 * R :])
+    def global_grads(i, carry):
+        kept = []
+        for h in (4 * i, 4 * i + 1, 4 * i + 2, 4 * i + 3):
+            out = attn[h]
+            up = ct_ref[:, head_cols(h)].astype(F32) * gains[pl.ds(h, 1)]
+            grad = inverse[...] * up - out * coef[...]
+            slope = inverse[...] * up_sums[h] - coef[...] * out_sums[h]
+            queries = q_t[h].astype(F32)
+            both_t = jnp.concatenate([queries * inverse_t, queries * coef_t], 1).astype(BF)
+            kept.append((h, grad, slope, both_t, (grad * f_s[3, h]).astype(BF).T))
+        both_t = jnp.concatenate([k[3] for k in kept], 1)
+        grad_t = jnp.concatenate([k[4] for k in kept], 1)
+        x = xs[pl.ds(4 * i, 4)].reshape(8 * R, G)
+        e = expo[pl.ds(4 * i, 4), :, 6 * R :].reshape(4 * R, G)
+        d_keys, d_values = nn(both_t, x), nn(grad_t, e)
+        dks[:, 6 * R :] += d_keys
+        dvs[:, 6 * R :] += d_values
+        for h, grad, slope, _, _ in kept:
+            d_attn[h], diag[h] = grad, slope
         return carry
 
     def send_grads(b):
@@ -377,18 +404,17 @@
             [remote(grad_out.at[b], grad_in.at[b], gr_send.at[b], gr_recv.at[b], partners[b])]
         )
 
-    lax.fori_loop(0, H, global_grads, 0, unroll=2)
+    lax.fori_loop(0, H // 4, global_grads, 0)
     d_global = jnp.concatenate([dks[:, 6 * R :] * SCALE, dvs[:, 6 * R :]], 0).astype(BF).T
     ga[1] = d_global.reshape(8, G // 8, 2 * HD)
     plane1 = started(plane_stage(1))
-    backward_group(2, (5, 3), True)
-    sent = send_grads(4)
+    backward_group(2, (5, 4), True)
+    sent = send_grads(4) + send_grads(3)
     waited(plane1)
     add_plane(1)
     z1 = started(z_stage(1))
-    sent += send_grads(2)
-    backward_group(1, (4, 2))
-    sent += send_grads(3) + send_grads(1)
+    backward_group(1, (3, 2))
+    sent += send_grads(2) + send_grads(1)
     waited(z1)
     add_z(1)
     back1 = started(plane_back(1))
@@ -407,10 +433,11 @@
     for b in range(5):
         d_keys = d_keys + grad_in[b, 0].astype(F32)
         d_values = d_values + grad_in[b, 1].astype(F32)
+    d_keys, d_values = d_keys.T, d_values.T
     waited(back1)
     back = nn(chosen, full[1].reshape(G, 2 * HD))
-    dk_ref[...] = (d_keys.T + back[:, :HD]).astype(BF)
-    dv_ref[...] = (d_values.T + back[:, HD:]).astype(BF)
+    dk_ref[...] = (d_keys + back[:, :HD]).astype(BF)
+    dv_ref[...] = (d_values + back[:, HD:]).astype(BF)
 
 
 def hand_over(*refs):

time: 55.7 us -> 52.8 us (0.948)
  Pallas kernels: 54.9 us -> 52 us
    pallas_call x1, Pallas kernels: 53.9 us -> 51 us  [per_device(): pl.pallas_call(kernel, out_shape=(jax.ShapeDtypeStruct(queries.shape, BF)...]
where the time goes in v5:
time: 52.8 us; the launch traced here: 52.7 us
  Pallas kernels  52 us (98%)
  between operations  0.64 us (1%)
    pallas_call x1, Pallas kernels, per_device(): pl.pallas_call(kernel, out_shape=(jax.ShapeDtypeStruct(queries.shape, BF)...  51 us

profile of v5, /device:TPU:1, one launch (start us, length us, event | category | flops | bytes accessed | tf_op | source)
XLA Modules:
  0.0 52.7 jit_solution(4023035975193240772)
XLA Ops:
  0.6 51.0 %butterfly.1 = (bf16[256,1024]{1,0:T(8,128)(2,1)S(1)}, bf16[256,1024]{1,0:T(8,128)(2,1)S(1)}, bf16[256,128]{1,0:T(8,128)(2,1)S(1)}, bf16[256,128]{1,0:T(8,128)(2,1)S(1)}) custom-call(bf16[256,1024]{1,0:T(8,128)(2,1)} %q_hbm.1, bf16[256,128]{1,0:T(8,128)(2,1)} %k_hbm.1, bf16[256,128]{1,0:T(8,128)(2,1)} %v_hbm.1, s32[1,256]{1,0:T(1,128)} %bitcast.5, ...), custom_call_target="tpu_custom_call" | custom-call | tf_op jit(solution)/shard_map/butterfly/pallas_call | solution.py:499
  51.6 1.0 %hand_over.1 = (bf16[256,1024]{1,0:T(8,128)(2,1)}, bf16[256,1024]{1,0:T(8,128)(2,1)}, bf16[256,128]{1,0:T(8,128)(2,1)}, bf16[256,128]{1,0:T(8,128)(2,1)}) custom-call(bf16[256,1024]{1,0:T(8,128)(2,1)S(1)} %get-tuple-element.8.refs_0_, bf16[256,1024]{1,0:T(8,128)(2,1)S(1)} %get-tuple-element.9.refs_1_, bf16[256,128]{1,0:T(8,128)(2,1)S(1)} %get-tuple-element.10.refs_2_, ...), custom_call_target="tpu_custom_call" | custom-call | tf_op jit(solution)/shard_map/hand_over/pallas_call | solution.py:529

commit v6 on v5

--- a/solution.py
+++ b/solution.py
@@ -88,18 +88,23 @@
         )
 
     barrier = pltpu.get_barrier_semaphore()
-    across = [
-        {"zh": lax.div(p, 4), "z": lax.rem(p, 4)}
-        for p in (lax.rem(zh * 4 + z + 1, 8), lax.rem(zh * 4 + z + 7, 8))
-    ]
+    at_end = 1 - lax.div(z * (3 - z), 2)
+    across = {"zh": 1 - zh, "z": 3 - z}
     y_peers = [{"y": lax.rem(y + o, 4)} for o in (1, 2, 3)]
-    near = plane_peers + [{"z": p} for p in z_peers] + y_peers + across
+    y_near = [y_peers[0], y_peers[2]]
+    near = plane_peers + [{"z": p} for p in z_peers] + y_near
 
     def signal_all(sem, peers):
         for peer in peers:
             pl.semaphore_signal(sem, inc=1, device_id=peer, device_id_type=pl.DeviceIdType.MESH)
 
+    def signal_across(sem):
+        @pl.when(at_end == 1)
+        def _():
+            signal_all(sem, [across])
+
     signal_all(barrier, near)
+    signal_across(barrier)
     inputs = [
         pltpu.make_async_copy(src, dst, in_sems.at[i])
         for i, (src, dst) in enumerate(
@@ -128,8 +133,9 @@
     ks[0:R] = k_ref[...]
     vs[0:R] = v_ref[...]
 
-    pl.semaphore_wait(barrier, len(near))
-    signal_all(ring_sem, across)
+    pl.semaphore_wait(barrier, len(near) + at_end)
+    signal_all(ring_sem, y_near)
+    signal_across(ring_sem)
 
     def kv_copies(b):
         lower = R * (b + 1)
@@ -268,7 +274,7 @@
     gains[...] = gain_ref[...].astype(F32)
     waited(kv[0])
     forward_group(0, block_bias(1))
-    pl.semaphore_wait(ring_sem, 2)
+    pl.semaphore_wait(ring_sem, 2 + at_end)
     waited(plane0)
     add_plane(0)
     keep_plane = fl[0]

time: 52.8 us -> 52.8 us (level)
  no operation moved by 1% of the time
where the time goes in v6:
time: 52.8 us; the launch traced here: 52.7 us
  Pallas kernels  52 us (98%)
  between operations  0.64 us (1%)
    pallas_call x1, Pallas kernels, per_device(): pl.pallas_call(kernel, out_shape=(jax.ShapeDtypeStruct(queries.shape, BF)...  51 us

profile of v6, /device:TPU:1, one launch (start us, length us, event | category | flops | bytes accessed | tf_op | source)
XLA Modules:
  0.0 52.7 jit_solution(11522438344165631201)
XLA Ops:
  0.6 51.0 %butterfly.1 = (bf16[256,1024]{1,0:T(8,128)(2,1)S(1)}, bf16[256,1024]{1,0:T(8,128)(2,1)S(1)}, bf16[256,128]{1,0:T(8,128)(2,1)S(1)}, bf16[256,128]{1,0:T(8,128)(2,1)S(1)}) custom-call(bf16[256,1024]{1,0:T(8,128)(2,1)} %q_hbm.1, bf16[256,128]{1,0:T(8,128)(2,1)} %k_hbm.1, bf16[256,128]{1,0:T(8,128)(2,1)} %v_hbm.1, s32[1,256]{1,0:T(1,128)} %bitcast.5, ...), custom_call_target="tpu_custom_call" | custom-call | tf_op jit(solution)/shard_map/butterfly/pallas_call | solution.py:505
  51.6 1.0 %hand_over.1 = (bf16[256,1024]{1,0:T(8,128)(2,1)}, bf16[256,1024]{1,0:T(8,128)(2,1)}, bf16[256,128]{1,0:T(8,128)(2,1)}, bf16[256,128]{1,0:T(8,128)(2,1)}) custom-call(bf16[256,1024]{1,0:T(8,128)(2,1)S(1)} %get-tuple-element.8.refs_0_, bf16[256,1024]{1,0:T(8,128)(2,1)S(1)} %get-tuple-element.9.refs_1_, bf16[256,128]{1,0:T(8,128)(2,1)S(1)} %get-tuple-element.10.refs_2_, ...), custom_call_target="tpu_custom_call" | custom-call | tf_op jit(solution)/shard_map/hand_over/pallas_call | solution.py:535
